TPU v7x, 32 devices: a whole 2x2x4 slice. The times are simulated.
32 devices in a mesh: fx: 8 (over z, x), fy: 4 (over y, core).
Axes of the slice: x: 2, y: 2, z: 4, core: 2. Of those that a mesh axis runs over, the one named last changes fastest.
Arguments:
- sky_image: float32 [16, 16384], P('fy', 'fx'), may hold values from -6 to 6
- col_off: int32 [8], replicated, may hold values from 0 to 16383
- row_off: int32 [4], replicated, may hold values from 0 to 65535
- layer_counts: int32 [8, 4], P('fx', 'fy'), may hold values from 1 to 8
- w_steps: int32 [8, 4, 8], P('fx', 'fy'), may hold values from 1 to 4
- live_blocks: int32 [8, 4], P('fx', 'fy'), may hold values from 1 to 16
- block_codes: int32 [8, 4, 16], P('fx', 'fy'), may hold values from 0 to 839
- vis_coords: float32 [8, 4, 16, 2, 128], P('fx', 'fy'), may hold values from 0 to 1
Outputs:
- visibilities: float32 [8, 4, 16, 2, 128], P('fx', 'fy')
All inputs are finite; a program needn't handle non-finite values.
Results may differ from a plain program's by a relative error of at most 0.018.
Values may be sent and summed in bfloat16 or wider, within the bound.
No kernel may reach another device: no remote copies, remote signals or barrier semaphores. Data moves between devices by JAX's collectives and lax.ppermute only.
A program may use at most 64 MiB of HBM per device.

v0:
```python
import functools
import math

import jax
import jax.numpy as jnp
from jax import lax
from jax.experimental import pallas as pl
from jax.experimental.pallas import tpu as pltpu
from jax.sharding import PartitionSpec as P

SG = 1024
NSKY = 65536

LANES = 128
FINE = 16

COS_POLY = (
    0.9999999890590228,
    -19.73920449945383,
    64.93911745989081,
    -85.45013953079767,
    60.167630950263465,
    -25.967599245923743,
    6.52865815775625,
)
SIN_POLY = (
    6.283184916495428,
    -41.34158923268831,
    81.59994332977429,
    -76.61447253115396,
    41.34288235413569,
    -12.471243534350362,
)


def horner(coefficients, value):
    total = jnp.full_like(value, coefficients[-1])
    for coefficient in coefficients[-2::-1]:
        total = total * value + coefficient
    return total


def turn(fraction):
    square = fraction * fraction
    return horner(COS_POLY, square), fraction * horner(SIN_POLY, square)


def turn_of_int(count, modulus):
    half = modulus // 2
    centred = ((count + half) & (modulus - 1)) - half
    return turn(centred.astype(jnp.float32) * (1.0 / modulus))


def wrap(value):
    return value - jnp.round(value)


def iota(shape, axis):
    return lax.broadcasted_iota(jnp.int32, shape, axis)


def column_tables_kernel(dims, col_off, first, twiddle, second):
    half_z, facet_rows, fine_cols, total_cols, wide, scale = dims
    here = lax.axis_index("fx")
    for target in range(2):
        offset = col_off[here ^ target]
        residue = offset + iota((facet_rows, LANES), 1)
        for slot in range(half_z):
            row = facet_rows * (here ^ (2 * slot)) + iota((facet_rows, LANES), 0)
            cosine, sine = turn_of_int(row * residue, LANES)
            rows = pl.ds(slot * facet_rows, facet_rows)
            first[rows, pl.ds(target * LANES, LANES)] = cosine.astype(jnp.bfloat16)
            first[rows, pl.ds((2 + target) * LANES, LANES)] = (-sine).astype(jnp.bfloat16)
        phase = iota((fine_cols, LANES), 0) * (offset + iota((fine_cols, LANES), 1))
        cosine, sine = turn_of_int(phase, total_cols)
        cols = pl.ds(target * LANES, LANES)
        twiddle[0, :, cols] = cosine * scale
        twiddle[1, :, cols] = sine * (-scale)
    cosine, sine = turn_of_int(iota((wide, fine_cols), 0) * iota((wide, fine_cols), 1), fine_cols)
    second[pl.ds(0, wide), pl.ds(0, fine_cols)] = cosine.astype(jnp.bfloat16)
    second[pl.ds(0, wide), pl.ds(fine_cols, fine_cols)] = sine.astype(jnp.bfloat16)
    second[pl.ds(wide, wide), pl.ds(0, fine_cols)] = (-sine).astype(jnp.bfloat16)
    second[pl.ds(wide, wide), pl.ds(fine_cols, fine_cols)] = cosine.astype(jnp.bfloat16)


def band_kernel(dims, *refs):
    half_z, facet_rows, fine_cols, rows_here = dims
    pieces = refs[:half_z]
    first, twiddle, second, own_out, other_out = refs[half_z:]
    stacked = jnp.concatenate(
        [
            jnp.concatenate([piece[row] for piece in pieces], axis=0)
            for row in range(rows_here)
        ],
        axis=1,
    )
    spread = lax.dot_general(
        stacked, first[...], (((0,), (0,)), ((), ())), preferred_element_type=jnp.float32
    )
    twist_real = twiddle[0]
    twist_imag = twiddle[1]
    for row in range(rows_here):
        part = spread[row * fine_cols : (row + 1) * fine_cols]
        part_real = part[:, : 2 * LANES]
        part_imag = part[:, 2 * LANES :]
        turned = jnp.concatenate(
            [
                part_real * twist_real - part_imag * twist_imag,
                part_real * twist_imag + part_imag * twist_real,
            ],
            axis=0,
        ).astype(jnp.bfloat16)
        bands = jnp.dot(second[...], turned, preferred_element_type=jnp.float32)
        bands = bands.astype(jnp.bfloat16)
        own_out[row] = bands[:, :LANES]
        other_out[row] = bands[:, LANES:]


def vis_tables_kernel(
    dims, row_off, counts, steps, codes, coords, rows_out, cols_out, kernels, coarse_out, u_out
):
    half_y, rows_here, num_rows, rows_grid, cols_grid, blocks, row_scale, vis_scale = dims
    here = lax.axis_index("fy")
    taps = 4 * half_y * rows_here
    order = iota((rows_grid, taps), 1)
    imag_in = order & 1
    cell = (order // 2) % rows_here
    slot = order // (2 * rows_here)
    owner = here ^ (2 * (slot % half_y)) ^ (slot // half_y)
    sky_row = owner * (NSKY // num_rows) + cell
    wave = row_off[here] + iota((rows_grid, taps), 0)
    cosine, sine = turn_of_int(sky_row * (wave & (NSKY - 1)), NSKY)
    cosine = cosine * row_scale
    sine = sine * row_scale
    rows_out[pl.ds(0, rows_grid), :] = jnp.where(imag_in == 0, cosine, sine).astype(jnp.bfloat16)
    rows_out[pl.ds(rows_grid, rows_grid), :] = jnp.where(imag_in == 0, -sine, cosine).astype(
        jnp.bfloat16
    )
    layers = steps.shape[2]
    depths = []
    depth = steps[0, 0, 0]
    for layer in range(layers):
        if layer:
            depth = depth + steps[0, 0, layer]
        depths.append(depth)
    centre = iota((1, cols_grid), 1) - cols_grid // 2
    squares = centre * centre
    phases = jnp.concatenate([depth * squares for depth in depths], axis=0)
    cosine, sine = turn_of_int(phases, 2 * cols_grid)
    cols_out[0] = cosine
    cols_out[1] = sine
    coarse_count = cols_grid // LANES
    mids = LANES // FINE
    row_index = iota((rows_grid, LANES), 0)
    row_centre = row_index - rows_grid // 2
    row_squares = row_centre * row_centre
    for block in range(blocks):
        plane = lax.rem(codes[0, 0, block], counts[0, 0])
        depth = depths[0]
        for layer in range(1, layers):
            depth = jnp.where(plane >= layer, depths[layer], depth)
        u_pos = coords[0, 0, block, pl.ds(0, 1), :]
        v_pos = coords[0, 0, block, pl.ds(1, 1), :]
        half = cols_grid
        screen = ((depth * row_squares + half) & (2 * cols_grid - 1)) - half
        angle = wrap(row_index.astype(jnp.float32) * u_pos) + screen.astype(jnp.float32) * (
            1.0 / (2 * cols_grid)
        )
        cosine, sine = turn(wrap(angle))
        u_out[block, 0] = cosine * vis_scale
        u_out[block, 1] = sine * vis_scale
        steps_wide = iota((coarse_count, LANES), 0).astype(jnp.float32)
        cosine, sine = turn(wrap(steps_wide * wrap(v_pos * float(LANES))))
        coarse_out[block, 0] = cosine
        coarse_out[block, 1] = sine
        steps_mid = iota((mids, LANES), 0).astype(jnp.float32)
        mid_cos, mid_sin = turn(wrap(steps_mid * wrap(v_pos * float(FINE))))
        steps_fine = iota((FINE, LANES), 0).astype(jnp.float32)
        fine_cos, fine_sin = turn(wrap(steps_fine * v_pos))
        for mid in range(mids):
            head_cos = mid_cos[mid : mid + 1]
            head_sin = mid_sin[mid : mid + 1]
            real = (head_cos * fine_cos - head_sin * fine_sin).astype(jnp.bfloat16)
            imag = (head_sin * fine_cos + head_cos * fine_sin).astype(jnp.bfloat16)
            upper = pl.ds(mid * FINE, FINE)
            lower = pl.ds(LANES + mid * FINE, FINE)
            kernels[block, upper, pl.ds(0, LANES)] = real
            kernels[block, upper, pl.ds(LANES, LANES)] = imag
            kernels[block, lower, pl.ds(0, LANES)] = -imag
            kernels[block, lower, pl.ds(LANES, LANES)] = real


def degrid_kernel(
    dims, counts, live, codes, own, other, rows_tab, cols_tab, kernels, coarse, u_tab, out,
    strips, layers_ref,
):
    half_y, rows_here, rows_grid, cols_grid, blocks, layers = dims
    wide = cols_grid // LANES
    per_slot = rows_here * 2 * wide
    for slot in range(half_y):
        strips[pl.ds(slot * per_slot, per_slot), :] = (
            own[slot].astype(jnp.float32).reshape(per_slot, LANES)
        )
        strips[pl.ds((half_y + slot) * per_slot, per_slot), :] = (
            other[slot].astype(jnp.float32).reshape(per_slot, LANES)
        )
    taps = 4 * half_y * rows_here
    for part in range(wide):
        source = strips[pl.ds(part, taps, stride=wide), :].astype(jnp.bfloat16)
        grid = jnp.dot(rows_tab[...], source, preferred_element_type=jnp.float32)
        grid_real = grid[:rows_grid]
        grid_imag = grid[rows_grid:]
        cols = pl.ds(part * LANES, LANES)
        rows = pl.ds(part * rows_grid, rows_grid)
        for layer in range(layers):
            cosine = cols_tab[0, pl.ds(layer, 1), cols]
            sine = cols_tab[1, pl.ds(layer, 1), cols]
            layers_ref[layer, rows, pl.ds(0, LANES)] = (
                grid_real * cosine - grid_imag * sine
            ).astype(jnp.bfloat16)
            layers_ref[layer, rows, pl.ds(LANES, LANES)] = (
                grid_real * sine + grid_imag * cosine
            ).astype(jnp.bfloat16)
    for block in range(blocks):
        plane = lax.rem(codes[0, 0, block], counts[0, 0])
        sums = jnp.dot(layers_ref[plane], kernels[block], preferred_element_type=jnp.float32)
        total_real = jnp.zeros((rows_grid, LANES), jnp.float32)
        total_imag = jnp.zeros((rows_grid, LANES), jnp.float32)
        for part in range(wide):
            sum_real = sums[part * rows_grid : (part + 1) * rows_grid, :LANES]
            sum_imag = sums[part * rows_grid : (part + 1) * rows_grid, LANES:]
            cosine = coarse[block, 0, pl.ds(part, 1), :]
            sine = coarse[block, 1, pl.ds(part, 1), :]
            total_real = total_real + (sum_real * cosine - sum_imag * sine)
            total_imag = total_imag + (sum_real * sine + sum_imag * cosine)
        u_cos = u_tab[block, 0]
        u_sin = u_tab[block, 1]
        vis_real = jnp.sum(u_cos * total_real - u_sin * total_imag, axis=0, keepdims=True)
        vis_imag = jnp.sum(u_cos * total_imag + u_sin * total_real, axis=0, keepdims=True)
        keep = block < live[0, 0]
        out[0, 0, block, pl.ds(0, 1), :] = jnp.where(keep, vis_real, 0.0)
        out[0, 0, block, pl.ds(1, 1), :] = jnp.where(keep, vis_imag, 0.0)


def in_smem():
    return pl.BlockSpec(memory_space=pltpu.SMEM)


def in_vmem():
    return pl.BlockSpec(memory_space=pltpu.VMEM)


def per_device(
    sky_image, col_off, row_off, layer_counts, w_steps, live_blocks, block_codes, vis_coords
):
    rows_here, facet_cols = sky_image.shape
    num_cols = lax.axis_size("fx")
    num_rows = lax.axis_size("fy")
    half_z = num_cols // 2
    half_y = num_rows // 2
    total_cols = facet_cols * num_cols
    total_rows = rows_here * num_rows
    rows_grid = total_rows
    fine_cols = total_cols // LANES
    facet_rows = facet_cols // fine_cols
    wide = SG // LANES
    blocks = block_codes.shape[2]
    vis_count = vis_coords.shape[-1]
    layers = w_steps.shape[2]
    f32, bf16 = jnp.float32, jnp.bfloat16

    def exchange(value, flip):
        pairs = [(i, i ^ flip) for i in range(num_cols * num_rows)]
        return lax.ppermute(value, ("fx", "fy"), pairs)

    own_sky = sky_image.astype(bf16).reshape(rows_here, facet_rows, fine_cols)
    pieces = [own_sky]
    for slot in range(1, half_z):
        pieces.append(exchange(own_sky, 2 * slot * num_rows))

    first, twiddle, second = pl.pallas_call(
        functools.partial(
            column_tables_kernel,
            (half_z, facet_rows, fine_cols, total_cols, wide, 1.0 / math.sqrt(total_cols)),
        ),
        name="column_tables",
        out_shape=(
            jax.ShapeDtypeStruct((half_z * facet_rows, 4 * LANES), bf16),
            jax.ShapeDtypeStruct((2, fine_cols, 2 * LANES), f32),
            jax.ShapeDtypeStruct((2 * wide, 2 * fine_cols), bf16),
        ),
        in_specs=[in_smem()],
        out_specs=(in_vmem(),) * 3,
    )(col_off)

    taps = 2 * total_rows
    rows_tab, cols_tab, kernels, coarse, u_tab = pl.pallas_call(
        functools.partial(
            vis_tables_kernel,
            (
                half_y,
                rows_here,
                num_rows,
                rows_grid,
                SG,
                blocks,
                1.0 / math.sqrt(total_rows),
                1.0 / math.sqrt(rows_grid * SG),
            ),
        ),
        name="vis_tables",
        out_shape=(
            jax.ShapeDtypeStruct((2 * rows_grid, taps), bf16),
            jax.ShapeDtypeStruct((2, layers, SG), f32),
            jax.ShapeDtypeStruct((blocks, 2 * LANES, 2 * vis_count), bf16),
            jax.ShapeDtypeStruct((blocks, 2, wide, vis_count), f32),
            jax.ShapeDtypeStruct((blocks, 2, rows_grid, vis_count), f32),
        ),
        in_specs=[in_smem()] * 4 + [in_vmem()],
        out_specs=(in_vmem(),) * 5,
    )(row_off, layer_counts, w_steps, block_codes, vis_coords)

    band_shape = jax.ShapeDtypeStruct((rows_here, 2 * wide, LANES), bf16)
    own_band, other_band = pl.pallas_call(
        functools.partial(band_kernel, (half_z, facet_rows, fine_cols, rows_here)),
        name="bands",
        out_shape=(band_shape, band_shape),
        in_specs=[in_vmem()] * (half_z + 3),
        out_specs=(in_vmem(),) * 2,
    )(*pieces, first, twiddle, second)

    strips = []
    for slot in range(half_y):
        near = exchange(own_band, 2 * slot) if slot else own_band
        far = exchange(other_band, num_rows + 2 * slot)
        strips.append((near.astype(f32) + far.astype(f32)).astype(bf16))
    own_strips = jnp.stack(strips)
    other_strips = exchange(own_strips, 1)

    return pl.pallas_call(
        functools.partial(
            degrid_kernel, (half_y, rows_here, rows_grid, SG, blocks, layers)
        ),
        name="degrid",
        out_shape=jax.ShapeDtypeStruct(vis_coords.shape, f32),
        in_specs=[in_smem()] * 3 + [in_vmem()] * 7,
        out_specs=in_vmem(),
        scratch_shapes=[
            pltpu.VMEM((2 * half_y * rows_here * 2 * wide, LANES), f32),
            pltpu.VMEM((layers, wide * rows_grid, 2 * LANES), bf16),
        ],
    )(
        layer_counts, live_blocks, block_codes, own_strips, other_strips,
        rows_tab, cols_tab, kernels, coarse, u_tab,
    )


def solution(mesh):
    placed = (
        P("fy", "fx"),
        P(),
        P(),
        P("fx", "fy"),
        P("fx", "fy", None),
        P("fx", "fy"),
        P("fx", "fy", None),
        P("fx", "fy", None, None, None),
    )
    return jax.shard_map(
        per_device,
        mesh=mesh,
        in_specs=placed,
        out_specs=P("fx", "fy", None, None, None),
        check_vma=False,
    )
```

profile of v0, /device:TPU:0, one launch (start us, length us, event | category | flops | bytes accessed | tf_op | source)
XLA Modules:
  0.0 28.3 jit_solution(1493101103867720426)
XLA Ops:
  0.0 0.8 %convert_bitcast_fusion = bf16[1,4,16,128]{3,1,2,0:T(4,128)(2,1)S(1)} fusion(f32[4,2048]{1,0:T(4,128)} %param.8), kind=kLoop, calls=%fused_computation.6 | loop fusion | flops 8192 | bytes 49152
  0.8 0.0 copy-start.1
  0.8 5.1 %collective-permute-start.2 = (bf16[4,16,128]{2,1,0:T(8,128)(2,1)S(1)}, bf16[4,16,128]{2,1,0:T(8,128)(2,1)S(1)}, u32[]{:S(2)}, u32[]{:S(2)}) collective-permute-start(bf16[4,16,128]{2,1,0:T(8,128)(2,1)S(1)} %bitcast.9), channel_id=1, source_target_pairs={{0,24},{1,25},{2,26},{3,27},{4,28},{5,29},{6,30},{7,31},{8,16},{9,... | collective-permute-start | bytes 49160 | tf_op jit(solution)/shard_map/ppermute | solution.py:274
  5.9 0.0 collective-permute-start.1
  5.9 0.6 %collective-permute-start = (bf16[4,16,128]{2,1,0:T(8,128)(2,1)S(1)}, bf16[4,16,128]{2,1,0:T(8,128)(2,1)S(1)}, u32[]{:S(2)}, u32[]{:S(2)}) collective-permute-start(bf16[4,16,128]{2,1,0:T(8,128)(2,1)S(1)} %bitcast.11), channel_id=1, source_target_pairs={{0,8},{1,9},{2,10},{3,11},{4,12},{5,13},{6,14},{7,15},{8,0},{9,1},... | collective-permute-start | bytes 49160 | tf_op jit(solution)/shard_map/ppermute | solution.py:274
  6.6 1.6 %column_tables.1 = (bf16[64,512]{1,0:T(8,128)(2,1)}, f32[2,128,256]{2,1,0:T(8,128)}, bf16[16,256]{1,0:T(8,128)(2,1)}) custom-call(s32[8]{0:T(128)} %col_off.1), custom_call_target="tpu_custom_call" | custom-call | tf_op jit(solution)/shard_map/column_tables/pallas_call | solution.py:281
  8.1 0.0 collective-permute-done.2.refs_3_
  8.1 2.4 %collective-permute-done.1.refs_2_ = bf16[4,16,128]{2,1,0:T(8,128)(2,1)S(1)} collective-permute-done((bf16[4,16,128]{2,1,0:T(8,128)(2,1)S(1)}, bf16[4,16,128]{2,1,0:T(8,128)(2,1)S(1)}, u32[]{:S(2)}, u32[]{:S(2)}) %collective-permute-start.1) | collective-permute-done | bytes 16416 | tf_op jit(solution)/shard_map/ppermute | solution.py:274
  10.6 0.0 collective-permute-done.refs_1_
  10.6 0.6 %copy-done.4 = bf16[4,16,128]{2,1,0:T(8,128)(2,1)} copy-done((bf16[4,16,128]{2,1,0:T(8,128)(2,1)}, bf16[4,16,128]{2,1,0:T(8,128)(2,1)S(1)}, u32[]{:S(2)}) %copy-start.4) | copy-done | bytes 16408
  11.2 2.1 %bands.1 = (bf16[4,16,128]{2,1,0:T(8,128)(2,1)}, bf16[4,16,128]{2,1,0:T(8,128)(2,1)}) custom-call(bf16[4,16,128]{2,1,0:T(8,128)(2,1)} %bitcast.12, bf16[4,16,128]{2,1,0:T(8,128)(2,1)} %copy-done.5, bf16[4,16,128]{2,1,0:T(8,128)(2,1)} %copy-done.4, bf16[4,16,128]{2,1,0:T(8,128)(2,1)} %copy-done.3, bf16[64,512]{1,0:T(8,128)(2,1)} %get-tuple-element.15.refs_4_, ...), custom_call_target="tpu_custom_call" | custom-call | tf_op jit(solution)/shard_map/bands/pallas_call | solution.py:324
  13.2 1.5 %collective-permute-start.3 = (bf16[4,16,128]{2,1,0:T(8,128)(2,1)}, bf16[4,16,128]{2,1,0:T(8,128)(2,1)S(1)}, u32[]{:S(2)}, u32[]{:S(2)}) collective-permute-start(bf16[4,16,128]{2,1,0:T(8,128)(2,1)} %get-tuple-element.19), channel_id=1, source_target_pairs={{0,4},{1,5},{2,6},{3,7},{4,0},{5,1},{6,2},{7,3},{8,12},{9,13},{10,... | collective-permute-start | bytes 49160 | tf_op jit(solution)/shard_map/ppermute | solution.py:274
  14.7 1.5 %collective-permute-start.5 = (bf16[4,16,128]{2,1,0:T(8,128)(2,1)}, bf16[4,16,128]{2,1,0:T(8,128)(2,1)S(1)}, u32[]{:S(2)}, u32[]{:S(2)}) collective-permute-start(bf16[4,16,128]{2,1,0:T(8,128)(2,1)} %get-tuple-element.19), channel_id=1, source_target_pairs={{0,6},{1,7},{2,4},{3,5},{4,2},{5,3},{6,0},{7,1},{8,14},{9,15},{10,... | collective-permute-start | bytes 49160 | tf_op jit(solution)/shard_map/ppermute | solution.py:274
  16.2 0.5 %collective-permute-start.4 = (bf16[4,16,128]{2,1,0:T(8,128)(2,1)}, bf16[4,16,128]{2,1,0:T(8,128)(2,1)S(1)}, u32[]{:S(2)}, u32[]{:S(2)}) collective-permute-start(bf16[4,16,128]{2,1,0:T(8,128)(2,1)} %get-tuple-element.18), channel_id=1, source_target_pairs={{0,2},{1,3},{2,0},{3,1},{4,6},{5,7},{6,4},{7,5},{8,10},{9,11},{10,... | collective-permute-start | bytes 49160 | tf_op jit(solution)/shard_map/ppermute | solution.py:274
  16.7 0.5 %collective-permute-done.3 = bf16[4,16,128]{2,1,0:T(8,128)(2,1)S(1)} collective-permute-done((bf16[4,16,128]{2,1,0:T(8,128)(2,1)}, bf16[4,16,128]{2,1,0:T(8,128)(2,1)S(1)}, u32[]{:S(2)}, u32[]{:S(2)}) %collective-permute-start.3) | collective-permute-done | bytes 16416 | tf_op jit(solution)/shard_map/ppermute | solution.py:274
  17.2 0.7 %fusion = bf16[1,4,16,128]{3,2,1,0:T(8,128)(2,1)S(1)} fusion(bf16[4,16,128]{2,1,0:T(8,128)(2,1)S(1)} %collective-permute-done.3, bf16[4,16,128]{2,1,0:T(8,128)(2,1)} %get-tuple-element.18), kind=kLoop, calls=%fused_computation.3 | loop fusion | flops 32768 | bytes 49152 | tf_op jit(solution)/shard_map/stack | solution.py:337
  17.9 2.3 %collective-permute-done.4 = bf16[4,16,128]{2,1,0:T(8,128)(2,1)S(1)} collective-permute-done((bf16[4,16,128]{2,1,0:T(8,128)(2,1)}, bf16[4,16,128]{2,1,0:T(8,128)(2,1)S(1)}, u32[]{:S(2)}, u32[]{:S(2)}) %collective-permute-start.4) | collective-permute-done | bytes 16416 | tf_op jit(solution)/shard_map/ppermute | solution.py:274
  20.2 0.0 collective-permute-done.5
  20.2 0.1 collective-permute-start.6
  21.6 3.0 %vis_tables.1 = (bf16[32,32]{1,0:T(8,128)(2,1)}, f32[2,8,1024]{2,1,0:T(8,128)}, bf16[16,256,256]{2,1,0:T(8,128)(2,1)}, f32[16,2,8,128]{3,2,1,0:T(8,128)}, f32[16,2,16,128]{3,2,1,0:T(8,128)}) custom-call(s32[4]{0:T(128)} %row_off.1, s32[1,1]{1,0:T(1,128)S(6)} %copy.12.counts, s32[1,1,8]{2,1,0:T(1,128)} %steps.1, s32[1,1,16]{2,1,0:T(1,128)} %codes.3, ...), custom_call_target="tpu_custom_call" | custom-call | tf_op jit(solution)/shard_map/vis_tables/pallas_call | solution.py:297
  24.6 0.0 collective-permute-done.6.other
  24.6 0.0 copy-done
  24.6 0.6 %copy-done.2 = bf16[2,4,16,128]{3,2,1,0:T(8,128)(2,1)} copy-done((bf16[2,4,16,128]{3,2,1,0:T(8,128)(2,1)}, bf16[2,4,16,128]{3,2,1,0:T(8,128)(2,1)S(1)}, u32[]{:S(2)}) %copy-start.2) | copy-done | bytes 32792
  25.2 3.2 %degrid.1 = f32[1,1,16,2,128]{4,3,2,1,0:T(2,128)} custom-call(s32[1,1]{1,0:T(1,128)S(6)} %copy.12.counts, s32[1,1]{1,0:T(1,128)S(6)} %copy.13.live, s32[1,1,16]{2,1,0:T(1,128)} %codes.3, bf16[2,4,16,128]{3,2,1,0:T(8,128)(2,1)} %copy-done, bf16[2,4,16,128]{3,2,1,0:T(8,128)(2,1)} %copy-done.2, bf16[32,32]{1,0:T(8,128)(2,1)} %get-tuple-element.20.rows_tab, ...), custom_call_target="tpu_custom_call" | custom-call | tf_op jit(solution)/shard_map/degrid/pallas_call | solution.py:340
  (11 shorter events, 0.0 us)
Async XLA Ops:
  0.8 9.8 %copy-start.1 = (bf16[1,4,16,128]{3,2,1,0:T(8,128)(2,1)}, bf16[1,4,16,128]{3,2,1,0:T(8,128)(2,1)S(1)}, u32[]{:S(2)}) copy-start(bf16[1,4,16,128]{3,2,1,0:T(8,128)(2,1)S(1)} %copy.11) | copy-start | bytes 49156
  0.8 7.3 %collective-permute-start.2 = (bf16[4,16,128]{2,1,0:T(8,128)(2,1)S(1)}, bf16[4,16,128]{2,1,0:T(8,128)(2,1)S(1)}, u32[]{:S(2)}, u32[]{:S(2)}) collective-permute-start(bf16[4,16,128]{2,1,0:T(8,128)(2,1)S(1)} %bitcast.9), channel_id=1, source_target_pairs={{0,24},{1,25},{2,26},{3,27},{4,28},{5,29},{6,30},{7,31},{8,16},{9,... | collective-permute-start | bytes 49160 | tf_op jit(solution)/shard_map/ppermute | solution.py:274
  5.9 4.6 %collective-permute-start.1 = (bf16[4,16,128]{2,1,0:T(8,128)(2,1)S(1)}, bf16[4,16,128]{2,1,0:T(8,128)(2,1)S(1)}, u32[]{:S(2)}, u32[]{:S(2)}) collective-permute-start(bf16[4,16,128]{2,1,0:T(8,128)(2,1)S(1)} %bitcast.10), channel_id=1, source_target_pairs={{0,16},{1,17},{2,18},{3,19},{4,20},{5,21},{6,22},{7,23},{8,24},{9,... | collective-permute-start | bytes 49160 | tf_op jit(solution)/shard_map/ppermute | solution.py:274
  5.9 4.6 %collective-permute-start = (bf16[4,16,128]{2,1,0:T(8,128)(2,1)S(1)}, bf16[4,16,128]{2,1,0:T(8,128)(2,1)S(1)}, u32[]{:S(2)}, u32[]{:S(2)}) collective-permute-start(bf16[4,16,128]{2,1,0:T(8,128)(2,1)S(1)} %bitcast.11), channel_id=1, source_target_pairs={{0,8},{1,9},{2,10},{3,11},{4,12},{5,13},{6,14},{7,15},{8,0},{9,1},... | collective-permute-start | bytes 49160 | tf_op jit(solution)/shard_map/ppermute | solution.py:274
  8.1 2.5 %copy-start.3 = (bf16[4,16,128]{2,1,0:T(8,128)(2,1)}, bf16[4,16,128]{2,1,0:T(8,128)(2,1)S(1)}, u32[]{:S(2)}) copy-start(bf16[4,16,128]{2,1,0:T(8,128)(2,1)S(1)} %collective-permute-done.2.refs_3_) | copy-start | bytes 49156
  10.6 0.6 %copy-start.4 = (bf16[4,16,128]{2,1,0:T(8,128)(2,1)}, bf16[4,16,128]{2,1,0:T(8,128)(2,1)S(1)}, u32[]{:S(2)}) copy-start(bf16[4,16,128]{2,1,0:T(8,128)(2,1)S(1)} %collective-permute-done.1.refs_2_) | copy-start | bytes 49156
  10.6 0.6 %copy-start.5 = (bf16[4,16,128]{2,1,0:T(8,128)(2,1)}, bf16[4,16,128]{2,1,0:T(8,128)(2,1)S(1)}, u32[]{:S(2)}) copy-start(bf16[4,16,128]{2,1,0:T(8,128)(2,1)S(1)} %collective-permute-done.refs_1_) | copy-start | bytes 49156
  13.2 3.9 %collective-permute-start.3 = (bf16[4,16,128]{2,1,0:T(8,128)(2,1)}, bf16[4,16,128]{2,1,0:T(8,128)(2,1)S(1)}, u32[]{:S(2)}, u32[]{:S(2)}) collective-permute-start(bf16[4,16,128]{2,1,0:T(8,128)(2,1)} %get-tuple-element.19), channel_id=1, source_target_pairs={{0,4},{1,5},{2,6},{3,7},{4,0},{5,1},{6,2},{7,3},{8,12},{9,13},{10,... | collective-permute-start | bytes 49160 | tf_op jit(solution)/shard_map/ppermute | solution.py:274
  14.7 5.4 %collective-permute-start.5 = (bf16[4,16,128]{2,1,0:T(8,128)(2,1)}, bf16[4,16,128]{2,1,0:T(8,128)(2,1)S(1)}, u32[]{:S(2)}, u32[]{:S(2)}) collective-permute-start(bf16[4,16,128]{2,1,0:T(8,128)(2,1)} %get-tuple-element.19), channel_id=1, source_target_pairs={{0,6},{1,7},{2,4},{3,5},{4,2},{5,3},{6,0},{7,1},{8,14},{9,15},{10,... | collective-permute-start | bytes 49160 | tf_op jit(solution)/shard_map/ppermute | solution.py:274
  16.2 3.9 %collective-permute-start.4 = (bf16[4,16,128]{2,1,0:T(8,128)(2,1)}, bf16[4,16,128]{2,1,0:T(8,128)(2,1)S(1)}, u32[]{:S(2)}, u32[]{:S(2)}) collective-permute-start(bf16[4,16,128]{2,1,0:T(8,128)(2,1)} %get-tuple-element.18), channel_id=1, source_target_pairs={{0,2},{1,3},{2,0},{3,1},{4,6},{5,7},{6,4},{7,5},{8,10},{9,11},{10,... | collective-permute-start | bytes 49160 | tf_op jit(solution)/shard_map/ppermute | solution.py:274
  20.2 4.4 %copy-start = (bf16[2,4,16,128]{3,2,1,0:T(8,128)(2,1)}, bf16[2,4,16,128]{3,2,1,0:T(8,128)(2,1)S(1)}, u32[]{:S(2)}) copy-start(bf16[2,4,16,128]{3,2,1,0:T(8,128)(2,1)S(1)} %pad_maximum_fusion.own) | copy-start | bytes 98308
  20.2 4.4 %collective-permute-start.6 = (bf16[2,4,16,128]{3,2,1,0:T(8,128)(2,1)S(1)}, bf16[2,4,16,128]{3,2,1,0:T(8,128)(2,1)S(1)}, u32[]{:S(2)}, u32[]{:S(2)}) collective-permute-start(bf16[2,4,16,128]{3,2,1,0:T(8,128)(2,1)S(1)} %pad_maximum_fusion.own), channel_id=1, source_target_pairs={{0,1},{1,0},{2,3},{3,2},{4,5},{5,4},{6,7},{7,6},{8,9},{9,8},{10,11... | collective-permute-start | bytes 98312 | tf_op jit(solution)/shard_map/ppermute | solution.py:274
  24.6 0.6 %copy-start.2 = (bf16[2,4,16,128]{3,2,1,0:T(8,128)(2,1)}, bf16[2,4,16,128]{3,2,1,0:T(8,128)(2,1)S(1)}, u32[]{:S(2)}) copy-start(bf16[2,4,16,128]{3,2,1,0:T(8,128)(2,1)S(1)} %collective-permute-done.6.other) | copy-start | bytes 98308
where the time goes:
time: 28.7 us; the launch traced here: 28.3 us
  Pallas kernels  9.77 us (34%)
  starting transfers between devices  9.34 us (33%)
  waiting for transfers between devices  5.16 us (18%)
  other arithmetic  1.5 us (5%)
  between operations  1.37 us (5%)
  local copies, waits for them, and re-layouts  1.19 us (4%)
    ppermute x7, starting transfers between devices, exchange(): return lax.ppermute(value, ('fx', 'fy'), pairs)  9.34 us
    ppermute x7, waiting for transfers between devices, exchange(): return lax.ppermute(value, ('fx', 'fy'), pairs)  5.16 us
    pallas_call x1, Pallas kernels, per_device(): pl.pallas_call(functools.partial(degrid_kernel, (half_y, rows_here, rows_...  3.17 us
    pallas_call x1, Pallas kernels, per_device(): pl.pallas_call(functools.partial(vis_tables_kernel, (half_y, rows_here, n...  2.99 us
    pallas_call x1, Pallas kernels, per_device(): pl.pallas_call(functools.partial(band_kernel, (half_z, facet_rows, fine_c...  2.06 us
    pallas_call x1, Pallas kernels, per_device(): pl.pallas_call(functools.partial(column_tables_kernel, (half_z, facet_row...  1.55 us
    unnamed x13, local copies, waits for them, and re-layouts  1.19 us
    unnamed x1, other arithmetic  0.76 us
  transfers between devices with their start and end apart: 7, of which 3 were waited for; matrix products, arithmetic and copies ran while one was open for 3% of the time, Pallas kernels for 16%

commit v1 on v0

--- a/solution.py
+++ b/solution.py
@@ -57,6 +57,32 @@
 
 def iota(shape, axis):
     return lax.broadcasted_iota(jnp.int32, shape, axis)
+
+
+def load_kernel(*refs):
+    count = (len(refs) - 3) // 2
+    sources, (sky_out, *targets) = refs[:count], refs[count : 2 * count]
+    landed, split, semaphores = refs[2 * count :]
+    copies = [
+        pltpu.make_async_copy(source, target, semaphores.at[index])
+        for index, (source, target) in enumerate(zip(sources, [landed, *targets]))
+    ]
+    for copy in copies:
+        copy.start()
+    copies[0].wait()
+    rows, pieces, width = sky_out.shape
+    parts = width // LANES
+    for piece in range(pieces):
+        for part in range(parts):
+            split[pl.ds(part * rows * pieces + piece, rows, stride=pieces), :] = landed[
+                :, pl.ds((piece * parts + part) * LANES, LANES)
+            ]
+    for row in range(rows):
+        for part in range(parts):
+            here = pl.ds((part * rows + row) * pieces, pieces)
+            sky_out[row, :, pl.ds(part * LANES, LANES)] = split[here, :].astype(jnp.bfloat16)
+    for copy in copies[1:]:
+        copy.wait()
 
 
 def column_tables_kernel(dims, col_off, first, twiddle, second):
@@ -117,10 +143,13 @@
 
 
 def vis_tables_kernel(
-    dims, row_off, counts, steps, codes, coords, rows_out, cols_out, kernels, coarse_out, u_out
+    dims, row_off, steps, codes, limits_in, coords,
+    rows_out, cols_out, kernels, coarse_out, u_out, planes, limits, semaphore,
 ):
     half_y, rows_here, num_rows, rows_grid, cols_grid, blocks, row_scale, vis_scale = dims
     here = lax.axis_index("fy")
+    fetch = pltpu.make_async_copy(limits_in, limits, semaphore)
+    fetch.start()
     taps = 4 * half_y * rows_here
     order = iota((rows_grid, taps), 1)
     imag_in = order & 1
@@ -149,13 +178,15 @@
     cosine, sine = turn_of_int(phases, 2 * cols_grid)
     cols_out[0] = cosine
     cols_out[1] = sine
+    fetch.wait()
     coarse_count = cols_grid // LANES
     mids = LANES // FINE
     row_index = iota((rows_grid, LANES), 0)
     row_centre = row_index - rows_grid // 2
     row_squares = row_centre * row_centre
     for block in range(blocks):
-        plane = lax.rem(codes[0, 0, block], counts[0, 0])
+        plane = lax.rem(codes[0, 0, block], limits[0, 0])
+        planes[block] = plane
         depth = depths[0]
         for layer in range(1, layers):
             depth = jnp.where(plane >= layer, depths[layer], depth)
@@ -167,8 +198,9 @@
             1.0 / (2 * cols_grid)
         )
         cosine, sine = turn(wrap(angle))
-        u_out[block, 0] = cosine * vis_scale
-        u_out[block, 1] = sine * vis_scale
+        weight = jnp.where(block < limits[0, 1], vis_scale, 0.0)
+        u_out[block, 0] = cosine * weight
+        u_out[block, 1] = sine * weight
         steps_wide = iota((coarse_count, LANES), 0).astype(jnp.float32)
         cosine, sine = turn(wrap(steps_wide * wrap(v_pos * float(LANES))))
         coarse_out[block, 0] = cosine
@@ -191,7 +223,7 @@
 
 
 def degrid_kernel(
-    dims, counts, live, codes, own, other, rows_tab, cols_tab, kernels, coarse, u_tab, out,
+    dims, planes, own, other, rows_tab, cols_tab, kernels, coarse, u_tab, out,
     strips, layers_ref,
 ):
     half_y, rows_here, rows_grid, cols_grid, blocks, layers = dims
@@ -222,8 +254,7 @@
                 grid_real * sine + grid_imag * cosine
             ).astype(jnp.bfloat16)
     for block in range(blocks):
-        plane = lax.rem(codes[0, 0, block], counts[0, 0])
-        sums = jnp.dot(layers_ref[plane], kernels[block], preferred_element_type=jnp.float32)
+        sums = jnp.dot(layers_ref[planes[block]], kernels[block], preferred_element_type=jnp.float32)
         total_real = jnp.zeros((rows_grid, LANES), jnp.float32)
         total_imag = jnp.zeros((rows_grid, LANES), jnp.float32)
         for part in range(wide):
@@ -237,9 +268,8 @@
         u_sin = u_tab[block, 1]
         vis_real = jnp.sum(u_cos * total_real - u_sin * total_imag, axis=0, keepdims=True)
         vis_imag = jnp.sum(u_cos * total_imag + u_sin * total_real, axis=0, keepdims=True)
-        keep = block < live[0, 0]
-        out[0, 0, block, pl.ds(0, 1), :] = jnp.where(keep, vis_real, 0.0)
-        out[0, 0, block, pl.ds(1, 1), :] = jnp.where(keep, vis_imag, 0.0)
+        out[0, 0, block, pl.ds(0, 1), :] = vis_real
+        out[0, 0, block, pl.ds(1, 1), :] = vis_imag
 
 
 def in_smem():
@@ -248,6 +278,13 @@
 
 def in_vmem():
     return pl.BlockSpec(memory_space=pltpu.VMEM)
+
+
+def kept(value):
+    return pltpu.with_memory_space_constraint(value, pltpu.VMEM)
+
+
+LIMIT = pltpu.CompilerParams(vmem_limit_bytes=16 << 20)
 
 
 def per_device(
@@ -273,7 +310,30 @@
         pairs = [(i, i ^ flip) for i in range(num_cols * num_rows)]
         return lax.ppermute(value, ("fx", "fy"), pairs)
 
-    own_sky = sky_image.astype(bf16).reshape(rows_here, facet_rows, fine_cols)
+    arguments = (
+        sky_image, vis_coords, col_off, row_off, w_steps, block_codes
+    )
+    own_sky, coords, *scalars = pl.pallas_call(
+        load_kernel,
+        name="load",
+        out_shape=(
+            pltpu.VMEM((rows_here, facet_rows, fine_cols), bf16),
+            pltpu.VMEM(vis_coords.shape, f32),
+            *(pltpu.SMEM(value.shape, value.dtype) for value in arguments[2:]),
+        ),
+        in_specs=[pl.BlockSpec(memory_space=pl.ANY)] * len(arguments),
+        out_specs=(in_vmem(),) * 2 + (in_smem(),) * (len(arguments) - 2),
+        scratch_shapes=[
+            pltpu.VMEM(sky_image.shape, f32),
+            pltpu.VMEM((rows_here * facet_cols // LANES, LANES), f32),
+            pltpu.SemaphoreType.DMA((len(arguments),)),
+        ],
+        compiler_params=LIMIT,
+    )(*(pltpu.with_memory_space_constraint(value, pltpu.HBM) for value in arguments))
+    coords = kept(coords)
+    col_off, row_off, w_steps, block_codes = (
+        pltpu.with_memory_space_constraint(value, pltpu.SMEM) for value in scalars
+    )
     pieces = [own_sky]
     for slot in range(1, half_z):
         pieces.append(exchange(own_sky, 2 * slot * num_rows))
@@ -285,16 +345,20 @@
         ),
         name="column_tables",
         out_shape=(
-            jax.ShapeDtypeStruct((half_z * facet_rows, 4 * LANES), bf16),
-            jax.ShapeDtypeStruct((2, fine_cols, 2 * LANES), f32),
-            jax.ShapeDtypeStruct((2 * wide, 2 * fine_cols), bf16),
+            pltpu.VMEM((half_z * facet_rows, 4 * LANES), bf16),
+            pltpu.VMEM((2, fine_cols, 2 * LANES), f32),
+            pltpu.VMEM((2 * wide, 2 * fine_cols), bf16),
         ),
         in_specs=[in_smem()],
         out_specs=(in_vmem(),) * 3,
+        compiler_params=LIMIT,
     )(col_off)
 
+    limits = jnp.where(
+        lax.broadcasted_iota(jnp.int32, (1, LANES), 1) == 0, layer_counts, live_blocks
+    )
     taps = 2 * total_rows
-    rows_tab, cols_tab, kernels, coarse, u_tab = pl.pallas_call(
+    *tables, planes = pl.pallas_call(
         functools.partial(
             vis_tables_kernel,
             (
@@ -310,30 +374,38 @@
         ),
         name="vis_tables",
         out_shape=(
-            jax.ShapeDtypeStruct((2 * rows_grid, taps), bf16),
-            jax.ShapeDtypeStruct((2, layers, SG), f32),
-            jax.ShapeDtypeStruct((blocks, 2 * LANES, 2 * vis_count), bf16),
-            jax.ShapeDtypeStruct((blocks, 2, wide, vis_count), f32),
-            jax.ShapeDtypeStruct((blocks, 2, rows_grid, vis_count), f32),
-        ),
-        in_specs=[in_smem()] * 4 + [in_vmem()],
-        out_specs=(in_vmem(),) * 5,
-    )(row_off, layer_counts, w_steps, block_codes, vis_coords)
-
-    band_shape = jax.ShapeDtypeStruct((rows_here, 2 * wide, LANES), bf16)
+            pltpu.VMEM((2 * rows_grid, taps), bf16),
+            pltpu.VMEM((2, layers, SG), f32),
+            pltpu.VMEM((blocks, 2 * LANES, 2 * vis_count), bf16),
+            pltpu.VMEM((blocks, 2, wide, vis_count), f32),
+            pltpu.VMEM((blocks, 2, rows_grid, vis_count), f32),
+            pltpu.SMEM((blocks,), jnp.int32),
+        ),
+        in_specs=[in_smem()] * 3 + [in_vmem()] * 2,
+        out_specs=(in_vmem(),) * 5 + (in_smem(),),
+        scratch_shapes=[pltpu.SMEM((1, LANES), jnp.int32), pltpu.SemaphoreType.DMA],
+        compiler_params=LIMIT,
+    )(row_off, w_steps, block_codes, kept(limits), coords)
+
+    band_shape = pltpu.VMEM((rows_here, 2 * wide, LANES), bf16)
     own_band, other_band = pl.pallas_call(
         functools.partial(band_kernel, (half_z, facet_rows, fine_cols, rows_here)),
         name="bands",
         out_shape=(band_shape, band_shape),
         in_specs=[in_vmem()] * (half_z + 3),
         out_specs=(in_vmem(),) * 2,
-    )(*pieces, first, twiddle, second)
-
-    strips = []
+        compiler_params=LIMIT,
+    )(*(kept(value) for value in (*pieces, first, twiddle, second)))
+
+    near, far = [own_band], []
     for slot in range(half_y):
-        near = exchange(own_band, 2 * slot) if slot else own_band
-        far = exchange(other_band, num_rows + 2 * slot)
-        strips.append((near.astype(f32) + far.astype(f32)).astype(bf16))
+        if slot:
+            near.append(exchange(own_band, 2 * slot))
+        far.append(exchange(other_band, num_rows + 2 * slot))
+    near, far, tables = lax.optimization_barrier((near, far, tables))
+    strips = [
+        (one.astype(f32) + two.astype(f32)).astype(bf16) for one, two in zip(near, far)
+    ]
     own_strips = jnp.stack(strips)
     other_strips = exchange(own_strips, 1)
 
@@ -343,15 +415,16 @@
         ),
         name="degrid",
         out_shape=jax.ShapeDtypeStruct(vis_coords.shape, f32),
-        in_specs=[in_smem()] * 3 + [in_vmem()] * 7,
+        in_specs=[in_smem()] + [in_vmem()] * 7,
         out_specs=in_vmem(),
         scratch_shapes=[
             pltpu.VMEM((2 * half_y * rows_here * 2 * wide, LANES), f32),
             pltpu.VMEM((layers, wide * rows_grid, 2 * LANES), bf16),
         ],
+        compiler_params=LIMIT,
     )(
-        layer_counts, live_blocks, block_codes, own_strips, other_strips,
-        rows_tab, cols_tab, kernels, coarse, u_tab,
+        pltpu.with_memory_space_constraint(planes, pltpu.SMEM),
+        *(kept(value) for value in (own_strips, other_strips, *tables)),
     )
 
 

time: 28.7 us -> 20.8 us (0.72)
  Pallas kernels: 9.77 us -> 4.34 us
  other arithmetic: 1.5 us -> 0.02 us
  local copies, waits for them, and re-layouts: 1.19 us -> 0 us
  waiting for transfers between devices: 5.16 us -> 5.49 us
    pallas_call x1, Pallas kernels: 3.17 us -> 1.42 us  [per_device(): pl.pallas_call(functools.partial(degrid_kernel, (half_y, rows_here, rows_...]
    pallas_call x1, Pallas kernels: 2.06 us -> 0.43 us  [per_device(): pl.pallas_call(functools.partial(band_kernel, (half_z, facet_rows, fine_c...]
    pallas_call x1, Pallas kernels: 2.99 us -> 1.37 us  [per_device(): pl.pallas_call(functools.partial(vis_tables_kernel, (half_y, rows_here, n...]
    pallas_call x1, Pallas kernels: 1.55 us -> 0.24 us  [per_device(): pl.pallas_call(functools.partial(column_tables_kernel, (half_z, facet_row...]
    unnamed x13 -> x0, local copies, waits for them, and re-layouts: 1.19 us -> none
    pallas_call x0 -> x1, Pallas kernels: none -> 0.87 us  [per_device(): pl.pallas_call(load_kernel, name='load', out_shape=(pltpu.VMEM((rows_here...]
    unnamed x1 -> x0, other arithmetic: 0.76 us -> none
    another operation x3 -> x2, other arithmetic: 0.74 us -> 0.02 us  [per_device(): own_strips = jnp.stack(strips)]
  transfers between devices with their start and end apart: 7 -> 7, of which waited for: 3 -> 3; matrix products, arithmetic and copies ran while one was open for 3% -> 0% of each run, Pallas kernels for 16% -> 8%
where the time goes in v1:
time: 20.8 us; the launch traced here: 20.6 us
  starting transfers between devices  9.37 us (45%)
  waiting for transfers between devices  5.49 us (26%)
  Pallas kernels  4.34 us (21%)
  between operations  1.36 us (7%)
    ppermute x7, starting transfers between devices, exchange(): return lax.ppermute(value, ('fx', 'fy'), pairs)  9.37 us
    ppermute x7, waiting for transfers between devices, exchange(): return lax.ppermute(value, ('fx', 'fy'), pairs)  5.49 us
    pallas_call x1, Pallas kernels, per_device(): pl.pallas_call(functools.partial(degrid_kernel, (half_y, rows_here, rows_...  1.42 us
    pallas_call x1, Pallas kernels, per_device(): pl.pallas_call(functools.partial(vis_tables_kernel, (half_y, rows_here, n...  1.37 us
    pallas_call x1, Pallas kernels, per_device(): pl.pallas_call(load_kernel, name='load', out_shape=(pltpu.VMEM((rows_here...  0.87 us
    pallas_call x1, Pallas kernels, per_device(): pl.pallas_call(functools.partial(band_kernel, (half_z, facet_rows, fine_c...  0.43 us
  transfers between devices with their start and end apart: 7, of which 3 were waited for; matrix products, arithmetic and copies ran while one was open for 0% of the time, Pallas kernels for 8%

profile of v1, /device:TPU:0, one launch (start us, length us, event | category | flops | bytes accessed | tf_op | source)
XLA Modules:
  0.0 20.6 jit_solution(12014694510368692141)
XLA Ops:
  0.0 0.9 %load.1 = (bf16[4,16,128]{2,1,0:T(8,128)(2,1)S(1)}, f32[1,1,16,2,128]{4,3,2,1,0:T(2,128)S(1)}, s32[8]{0:T(128)S(4)}, s32[4]{0:T(128)S(4)}, s32[1,1,8]{2,1,0:T(1,128)S(4)}, /*index=5*/s32[1,1,16]{2,1,0:T(1,128)S(4)}) custom-call(f32[4,2048]{1,0:T(4,128)} %refs_0_.1, f32[1,1,16,2,128]{4,3,2,1,0:T(2,128)} %refs_1_.1, s32[8]{0:T(128)} %refs_2_.1, s32[4]{0:T(128)} %refs_3_.1, ...), custom_call_target="tpu_custom_call" | custom-call | tf_op jit(solution)/shard_map/load/pallas_call | solution.py:316
  0.9 5.1 %collective-permute-start.2 = (bf16[4,16,128]{2,1,0:T(8,128)(2,1)S(1)}, bf16[4,16,128]{2,1,0:T(8,128)(2,1)S(1)}, u32[]{:S(2)}, u32[]{:S(2)}) collective-permute-start(bf16[4,16,128]{2,1,0:T(8,128)(2,1)S(1)} %get-tuple-element.36.refs_0_), channel_id=1, source_target_pairs={{0,24},{1,25},{2,26},{3,27},{4,28},{5,29},{6,30},{7,31},{8,16},{9,... | collective-permute-start | bytes 49160 | tf_op jit(solution)/shard_map/ppermute | solution.py:311
  6.0 0.0 collective-permute-start.1
  6.0 0.6 %collective-permute-start = (bf16[4,16,128]{2,1,0:T(8,128)(2,1)S(1)}, bf16[4,16,128]{2,1,0:T(8,128)(2,1)S(1)}, u32[]{:S(2)}, u32[]{:S(2)}) collective-permute-start(bf16[4,16,128]{2,1,0:T(8,128)(2,1)S(1)} %get-tuple-element.36.refs_0_), channel_id=1, source_target_pairs={{0,8},{1,9},{2,10},{3,11},{4,12},{5,13},{6,14},{7,15},{8,0},{9,1},... | collective-permute-start | bytes 49160 | tf_op jit(solution)/shard_map/ppermute | solution.py:311
  8.0 0.2 %column_tables.1 = (bf16[64,512]{1,0:T(8,128)(2,1)S(1)}, f32[2,128,256]{2,1,0:T(8,128)S(1)}, bf16[16,256]{1,0:T(8,128)(2,1)S(1)}) custom-call(s32[8]{0:T(128)S(4)} %get-tuple-element.37.col_off), custom_call_target="tpu_custom_call" | custom-call | tf_op jit(solution)/shard_map/column_tables/pallas_call | solution.py:341
  8.2 0.0 collective-permute-done.2.refs_3_
  8.2 2.4 %collective-permute-done.1.refs_2_ = bf16[4,16,128]{2,1,0:T(8,128)(2,1)S(1)} collective-permute-done((bf16[4,16,128]{2,1,0:T(8,128)(2,1)S(1)}, bf16[4,16,128]{2,1,0:T(8,128)(2,1)S(1)}, u32[]{:S(2)}, u32[]{:S(2)}) %collective-permute-start.1) | collective-permute-done | bytes 16416 | tf_op jit(solution)/shard_map/ppermute | solution.py:311
  10.7 0.0 collective-permute-done.refs_1_
  10.7 0.4 %bands.1 = (bf16[4,16,128]{2,1,0:T(8,128)(2,1)S(1)}, bf16[4,16,128]{2,1,0:T(8,128)(2,1)S(1)}) custom-call(bf16[4,16,128]{2,1,0:T(8,128)(2,1)S(1)} %get-tuple-element.36.refs_0_, bf16[4,16,128]{2,1,0:T(8,128)(2,1)S(1)} %collective-permute-done.refs_1_, bf16[4,16,128]{2,1,0:T(8,128)(2,1)S(1)} %collective-permute-done.1.refs_2_, ...), custom_call_target="tpu_custom_call" | custom-call | tf_op jit(solution)/shard_map/bands/pallas_call | solution.py:391
  11.1 2.5 %collective-permute-start.5 = (bf16[4,16,128]{2,1,0:T(8,128)(2,1)S(1)}, bf16[4,16,128]{2,1,0:T(8,128)(2,1)S(1)}, u32[]{:S(2)}, u32[]{:S(2)}) collective-permute-start(bf16[4,16,128]{2,1,0:T(8,128)(2,1)S(1)} %get-tuple-element.42), channel_id=1, source_target_pairs={{0,6},{1,7},{2,4},{3,5},{4,2},{5,3},{6,0},{7,1},{8,14},{9,15},{10,... | collective-permute-start | bytes 49160 | tf_op jit(solution)/shard_map/ppermute | solution.py:311
  13.6 0.5 %collective-permute-start.4 = (bf16[4,16,128]{2,1,0:T(8,128)(2,1)S(1)}, bf16[4,16,128]{2,1,0:T(8,128)(2,1)S(1)}, u32[]{:S(2)}, u32[]{:S(2)}) collective-permute-start(bf16[4,16,128]{2,1,0:T(8,128)(2,1)S(1)} %get-tuple-element.42), channel_id=1, source_target_pairs={{0,4},{1,5},{2,6},{3,7},{4,0},{5,1},{6,2},{7,3},{8,12},{9,13},{10,... | collective-permute-start | bytes 49160 | tf_op jit(solution)/shard_map/ppermute | solution.py:311
  14.1 0.5 %collective-permute-start.3 = (bf16[4,16,128]{2,1,0:T(8,128)(2,1)S(1)}, bf16[4,16,128]{2,1,0:T(8,128)(2,1)S(1)}, u32[]{:S(2)}, u32[]{:S(2)}) collective-permute-start(bf16[4,16,128]{2,1,0:T(8,128)(2,1)S(1)} %get-tuple-element.48), channel_id=1, source_target_pairs={{0,2},{1,3},{2,0},{3,1},{4,6},{5,7},{6,4},{7,5},{8,10},{9,11},{10,... | collective-permute-start | bytes 49160 | tf_op jit(solution)/shard_map/ppermute | solution.py:311
  14.6 1.4 %vis_tables.1 = (bf16[32,32]{1,0:T(8,128)(2,1)S(1)}, f32[2,8,1024]{2,1,0:T(8,128)S(1)}, bf16[16,256,256]{2,1,0:T(8,128)(2,1)S(1)}, f32[16,2,8,128]{3,2,1,0:T(8,1...) custom-call(s32[4]{0:T(128)S(4)} %get-tuple-element.31.row_off, s32[1,1,8]{2,1,0:T(1,128)S(4)} %get-tuple-element.32.steps, ...), custom_call_target="tpu_custom_call" | custom-call | tf_op jit(solution)/shard_map/vis_tables/pallas_call | solution.py:361
  16.0 1.8 %collective-permute-done.3 = bf16[4,16,128]{2,1,0:T(8,128)(2,1)S(1)} collective-permute-done((bf16[4,16,128]{2,1,0:T(8,128)(2,1)S(1)}, bf16[4,16,128]{2,1,0:T(8,128)(2,1)S(1)}, u32[]{:S(2)}, u32[]{:S(2)}) %collective-permute-start.3) | collective-permute-done | bytes 16416 | tf_op jit(solution)/shard_map/ppermute | solution.py:311
  17.9 0.0 collective-permute-done.5
  17.9 0.0 collective-permute-done.4
  17.9 0.1 collective-permute-start.6
  18.0 1.2 %collective-permute-done.6.other = bf16[2,4,16,128]{3,2,1,0:T(8,128)(2,1)S(1)} collective-permute-done((bf16[2,4,16,128]{3,2,1,0:T(8,128)(2,1)S(1)}, bf16[2,4,16,128]{3,2,1,0:T(8,128)(2,1)S(1)}, u32[]{:S(2)}, u32[]{:S(2)}) %collective-permute-start.6) | collective-permute-done | bytes 32800 | tf_op jit(solution)/shard_map/ppermute | solution.py:311
  19.2 1.4 %degrid.1 = f32[1,1,16,2,128]{4,3,2,1,0:T(2,128)} custom-call(s32[16]{0:T(128)S(4)} %get-tuple-element.35.planes, bf16[2,4,16,128]{3,2,1,0:T(8,128)(2,1)S(1)} %pad_maximum_fusion.own, bf16[2,4,16,128]{3,2,1,0:T(8,128)(2,1)S(1)} %collective-permute-done.6.other, bf16[32,32]{1,0:T(8,128)(2,1)S(1)} %get-tuple-element.52.rows_tab, ...), custom_call_target="tpu_custom_call" | custom-call | tf_op jit(solution)/shard_map/degrid/pallas_call | solution.py:412
  (3 shorter events, 0.0 us)
Async XLA Ops:
  0.9 7.3 %collective-permute-start.2 = (bf16[4,16,128]{2,1,0:T(8,128)(2,1)S(1)}, bf16[4,16,128]{2,1,0:T(8,128)(2,1)S(1)}, u32[]{:S(2)}, u32[]{:S(2)}) collective-permute-start(bf16[4,16,128]{2,1,0:T(8,128)(2,1)S(1)} %get-tuple-element.36.refs_0_), channel_id=1, source_target_pairs={{0,24},{1,25},{2,26},{3,27},{4,28},{5,29},{6,30},{7,31},{8,16},{9,... | collective-permute-start | bytes 49160 | tf_op jit(solution)/shard_map/ppermute | solution.py:311
  6.0 4.6 %collective-permute-start.1 = (bf16[4,16,128]{2,1,0:T(8,128)(2,1)S(1)}, bf16[4,16,128]{2,1,0:T(8,128)(2,1)S(1)}, u32[]{:S(2)}, u32[]{:S(2)}) collective-permute-start(bf16[4,16,128]{2,1,0:T(8,128)(2,1)S(1)} %get-tuple-element.36.refs_0_), channel_id=1, source_target_pairs={{0,16},{1,17},{2,18},{3,19},{4,20},{5,21},{6,22},{7,23},{8,24},{9,... | collective-permute-start | bytes 49160 | tf_op jit(solution)/shard_map/ppermute | solution.py:311
  6.0 4.6 %collective-permute-start = (bf16[4,16,128]{2,1,0:T(8,128)(2,1)S(1)}, bf16[4,16,128]{2,1,0:T(8,128)(2,1)S(1)}, u32[]{:S(2)}, u32[]{:S(2)}) collective-permute-start(bf16[4,16,128]{2,1,0:T(8,128)(2,1)S(1)} %get-tuple-element.36.refs_0_), channel_id=1, source_target_pairs={{0,8},{1,9},{2,10},{3,11},{4,12},{5,13},{6,14},{7,15},{8,0},{9,1},... | collective-permute-start | bytes 49160 | tf_op jit(solution)/shard_map/ppermute | solution.py:311
  11.1 6.8 %collective-permute-start.5 = (bf16[4,16,128]{2,1,0:T(8,128)(2,1)S(1)}, bf16[4,16,128]{2,1,0:T(8,128)(2,1)S(1)}, u32[]{:S(2)}, u32[]{:S(2)}) collective-permute-start(bf16[4,16,128]{2,1,0:T(8,128)(2,1)S(1)} %get-tuple-element.42), channel_id=1, source_target_pairs={{0,6},{1,7},{2,4},{3,5},{4,2},{5,3},{6,0},{7,1},{8,14},{9,15},{10,... | collective-permute-start | bytes 49160 | tf_op jit(solution)/shard_map/ppermute | solution.py:311
  13.6 4.3 %collective-permute-start.4 = (bf16[4,16,128]{2,1,0:T(8,128)(2,1)S(1)}, bf16[4,16,128]{2,1,0:T(8,128)(2,1)S(1)}, u32[]{:S(2)}, u32[]{:S(2)}) collective-permute-start(bf16[4,16,128]{2,1,0:T(8,128)(2,1)S(1)} %get-tuple-element.42), channel_id=1, source_target_pairs={{0,4},{1,5},{2,6},{3,7},{4,0},{5,1},{6,2},{7,3},{8,12},{9,13},{10,... | collective-permute-start | bytes 49160 | tf_op jit(solution)/shard_map/ppermute | solution.py:311
  14.1 3.7 %collective-permute-start.3 = (bf16[4,16,128]{2,1,0:T(8,128)(2,1)S(1)}, bf16[4,16,128]{2,1,0:T(8,128)(2,1)S(1)}, u32[]{:S(2)}, u32[]{:S(2)}) collective-permute-start(bf16[4,16,128]{2,1,0:T(8,128)(2,1)S(1)} %get-tuple-element.48), channel_id=1, source_target_pairs={{0,2},{1,3},{2,0},{3,1},{4,6},{5,7},{6,4},{7,5},{8,10},{9,11},{10,... | collective-permute-start | bytes 49160 | tf_op jit(solution)/shard_map/ppermute | solution.py:311
  17.9 1.3 %collective-permute-start.6 = (bf16[2,4,16,128]{3,2,1,0:T(8,128)(2,1)S(1)}, bf16[2,4,16,128]{3,2,1,0:T(8,128)(2,1)S(1)}, u32[]{:S(2)}, u32[]{:S(2)}) collective-permute-start(bf16[2,4,16,128]{3,2,1,0:T(8,128)(2,1)S(1)} %pad_maximum_fusion.own), channel_id=1, source_target_pairs={{0,1},{1,0},{2,3},{3,2},{4,5},{5,4},{6,7},{7,6},{8,9},{9,8},{10,11... | collective-permute-start | bytes 98312 | tf_op jit(solution)/shard_map/ppermute | solution.py:311

commit v2 on v1

--- a/solution.py
+++ b/solution.py
@@ -113,58 +113,56 @@
     half_z, facet_rows, fine_cols, rows_here = dims
     pieces = refs[:half_z]
     first, twiddle, second, own_out, other_out = refs[half_z:]
-    stacked = jnp.concatenate(
-        [
-            jnp.concatenate([piece[row] for piece in pieces], axis=0)
-            for row in range(rows_here)
-        ],
-        axis=1,
-    )
-    spread = lax.dot_general(
-        stacked, first[...], (((0,), (0,)), ((), ())), preferred_element_type=jnp.float32
-    )
     twist_real = twiddle[0]
     twist_imag = twiddle[1]
-    for row in range(rows_here):
-        part = spread[row * fine_cols : (row + 1) * fine_cols]
-        part_real = part[:, : 2 * LANES]
-        part_imag = part[:, 2 * LANES :]
-        turned = jnp.concatenate(
+    for held in range(2):
+        stacked = jnp.concatenate(
             [
-                part_real * twist_real - part_imag * twist_imag,
-                part_real * twist_imag + part_imag * twist_real,
+                jnp.concatenate([piece[held, row] for piece in pieces], axis=0)
+                for row in range(rows_here)
             ],
-            axis=0,
-        ).astype(jnp.bfloat16)
-        bands = jnp.dot(second[...], turned, preferred_element_type=jnp.float32)
-        bands = bands.astype(jnp.bfloat16)
-        own_out[row] = bands[:, :LANES]
-        other_out[row] = bands[:, LANES:]
+            axis=1,
+        )
+        spread = lax.dot_general(
+            stacked, first[...], (((0,), (0,)), ((), ())), preferred_element_type=jnp.float32
+        )
+        for row in range(rows_here):
+            part = spread[row * fine_cols : (row + 1) * fine_cols]
+            part_real = part[:, : 2 * LANES]
+            part_imag = part[:, 2 * LANES :]
+            turned = jnp.concatenate(
+                [
+                    part_real * twist_real - part_imag * twist_imag,
+                    part_real * twist_imag + part_imag * twist_real,
+                ],
+                axis=0,
+            ).astype(jnp.bfloat16)
+            bands = jnp.dot(second[...], turned, preferred_element_type=jnp.float32)
+            bands = bands.astype(jnp.bfloat16)
+            own_out[held, row] = bands[:, :LANES]
+            other_out[held, row] = bands[:, LANES:]
 
 
 def vis_tables_kernel(
     dims, row_off, steps, codes, limits_in, coords,
-    rows_out, cols_out, kernels, coarse_out, u_out, planes, limits, semaphore,
+    cols_out, kernels, coarse_out, rows_out, planes, limits, u_tab, semaphore,
 ):
     half_y, rows_here, num_rows, rows_grid, cols_grid, blocks, row_scale, vis_scale = dims
     here = lax.axis_index("fy")
     fetch = pltpu.make_async_copy(limits_in, limits, semaphore)
     fetch.start()
-    taps = 4 * half_y * rows_here
-    order = iota((rows_grid, taps), 1)
-    imag_in = order & 1
-    cell = (order // 2) % rows_here
-    slot = order // (2 * rows_here)
-    owner = here ^ (2 * (slot % half_y)) ^ (slot // half_y)
-    sky_row = owner * (NSKY // num_rows) + cell
-    wave = row_off[here] + iota((rows_grid, taps), 0)
+    shape = (2 * rows_grid, 2 * rows_grid)
+    order = iota(shape, 0)
+    imag_out = order // rows_grid
+    slot = (order // (2 * rows_here)) % half_y
+    owner = ((here | 1) ^ (2 * slot)) - (order // rows_here) % 2
+    sky_row = owner * (NSKY // num_rows) + order % rows_here
+    column = iota(shape, 1)
+    imag_in = column // rows_grid
+    wave = row_off[here] + column % rows_grid
     cosine, sine = turn_of_int(sky_row * (wave & (NSKY - 1)), NSKY)
-    cosine = cosine * row_scale
-    sine = sine * row_scale
-    rows_out[pl.ds(0, rows_grid), :] = jnp.where(imag_in == 0, cosine, sine).astype(jnp.bfloat16)
-    rows_out[pl.ds(rows_grid, rows_grid), :] = jnp.where(imag_in == 0, -sine, cosine).astype(
-        jnp.bfloat16
-    )
+    cross = jnp.where(imag_out == 0, sine, -sine)
+    row_weights = (jnp.where(imag_in == imag_out, cosine, cross) * row_scale).astype(jnp.bfloat16)
     layers = steps.shape[2]
     depths = []
     depth = steps[0, 0, 0]
@@ -199,8 +197,9 @@
         )
         cosine, sine = turn(wrap(angle))
         weight = jnp.where(block < limits[0, 1], vis_scale, 0.0)
-        u_out[block, 0] = cosine * weight
-        u_out[block, 1] = sine * weight
+        spot = pl.ds(block * LANES, LANES)
+        u_tab[pl.ds(0, rows_grid), spot] = (cosine * weight).astype(jnp.bfloat16)
+        u_tab[pl.ds(rows_grid, rows_grid), spot] = (sine * weight).astype(jnp.bfloat16)
         steps_wide = iota((coarse_count, LANES), 0).astype(jnp.float32)
         cosine, sine = turn(wrap(steps_wide * wrap(v_pos * float(LANES))))
         coarse_out[block, 0] = cosine
@@ -220,56 +219,66 @@
             kernels[block, upper, pl.ds(LANES, LANES)] = imag
             kernels[block, lower, pl.ds(0, LANES)] = -imag
             kernels[block, lower, pl.ds(LANES, LANES)] = real
+    weights = jnp.dot(row_weights, u_tab[...], preferred_element_type=jnp.float32)
+    for block in range(blocks):
+        for part in range(2):
+            rows_out[block, part] = weights[
+                part * rows_grid : (part + 1) * rows_grid, block * LANES : (block + 1) * LANES
+            ]
 
 
 def degrid_kernel(
-    dims, planes, own, other, rows_tab, cols_tab, kernels, coarse, u_tab, out,
-    strips, layers_ref,
+    dims, planes, local, passed, cols_tab, kernels, coarse, rows_tab, out, strips, layers_ref
 ):
-    half_y, rows_here, rows_grid, cols_grid, blocks, layers = dims
+    held, cols_grid, blocks, layers = dims
     wide = cols_grid // LANES
-    per_slot = rows_here * 2 * wide
-    for slot in range(half_y):
-        strips[pl.ds(slot * per_slot, per_slot), :] = (
-            own[slot].astype(jnp.float32).reshape(per_slot, LANES)
+    lead = lax.axis_index("fy") % 2 == 1
+    size = 2 * wide
+    for index in range(held):
+        spot = (index // (local.shape[1] * local.shape[2]),
+                index // local.shape[2] % local.shape[1], index % local.shape[2])
+        strips[pl.ds(index * size, size), :] = jnp.where(
+            lead, local[spot].astype(jnp.float32), passed[spot].astype(jnp.float32)
         )
-        strips[pl.ds((half_y + slot) * per_slot, per_slot), :] = (
-            other[slot].astype(jnp.float32).reshape(per_slot, LANES)
-        )
-    taps = 4 * half_y * rows_here
-    for part in range(wide):
-        source = strips[pl.ds(part, taps, stride=wide), :].astype(jnp.bfloat16)
-        grid = jnp.dot(rows_tab[...], source, preferred_element_type=jnp.float32)
-        grid_real = grid[:rows_grid]
-        grid_imag = grid[rows_grid:]
-        cols = pl.ds(part * LANES, LANES)
-        rows = pl.ds(part * rows_grid, rows_grid)
+    for part in range(0, wide, 2):
+        pair = []
+        for col in (part, part + 1):
+            real = strips[pl.ds(col, held, stride=2 * wide), :]
+            imag = strips[pl.ds(wide + col, held, stride=2 * wide), :]
+            pair.append((col, real, imag))
+        rows = pl.ds(part * held, 2 * held)
         for layer in range(layers):
-            cosine = cols_tab[0, pl.ds(layer, 1), cols]
-            sine = cols_tab[1, pl.ds(layer, 1), cols]
-            layers_ref[layer, rows, pl.ds(0, LANES)] = (
-                grid_real * cosine - grid_imag * sine
-            ).astype(jnp.bfloat16)
-            layers_ref[layer, rows, pl.ds(LANES, LANES)] = (
-                grid_real * sine + grid_imag * cosine
-            ).astype(jnp.bfloat16)
+            turned_real, turned_imag = [], []
+            for col, real, imag in pair:
+                cols = pl.ds(col * LANES, LANES)
+                cosine = cols_tab[0, pl.ds(layer, 1), cols]
+                sine = cols_tab[1, pl.ds(layer, 1), cols]
+                turned_real.append(real * cosine - imag * sine)
+                turned_imag.append(real * sine + imag * cosine)
+            layers_ref[layer, rows, pl.ds(0, LANES)] = jnp.concatenate(turned_real).astype(
+                jnp.bfloat16
+            )
+            layers_ref[layer, rows, pl.ds(LANES, LANES)] = jnp.concatenate(turned_imag).astype(
+                jnp.bfloat16
+            )
     for block in range(blocks):
         sums = jnp.dot(layers_ref[planes[block]], kernels[block], preferred_element_type=jnp.float32)
-        total_real = jnp.zeros((rows_grid, LANES), jnp.float32)
-        total_imag = jnp.zeros((rows_grid, LANES), jnp.float32)
+        total_real = jnp.zeros((held, LANES), jnp.float32)
+        total_imag = jnp.zeros((held, LANES), jnp.float32)
         for part in range(wide):
-            sum_real = sums[part * rows_grid : (part + 1) * rows_grid, :LANES]
-            sum_imag = sums[part * rows_grid : (part + 1) * rows_grid, LANES:]
+            sum_real = sums[part * held : (part + 1) * held, :LANES]
+            sum_imag = sums[part * held : (part + 1) * held, LANES:]
             cosine = coarse[block, 0, pl.ds(part, 1), :]
             sine = coarse[block, 1, pl.ds(part, 1), :]
             total_real = total_real + (sum_real * cosine - sum_imag * sine)
             total_imag = total_imag + (sum_real * sine + sum_imag * cosine)
-        u_cos = u_tab[block, 0]
-        u_sin = u_tab[block, 1]
-        vis_real = jnp.sum(u_cos * total_real - u_sin * total_imag, axis=0, keepdims=True)
-        vis_imag = jnp.sum(u_cos * total_imag + u_sin * total_real, axis=0, keepdims=True)
-        out[0, 0, block, pl.ds(0, 1), :] = vis_real
-        out[0, 0, block, pl.ds(1, 1), :] = vis_imag
+        row_cos = rows_tab[block, 0]
+        row_sin = rows_tab[block, 1]
+        vis_real = jnp.sum(row_cos * total_real - row_sin * total_imag, axis=0, keepdims=True)
+        vis_imag = jnp.sum(row_cos * total_imag + row_sin * total_real, axis=0, keepdims=True)
+        for part, value in enumerate((vis_real, vis_imag)):
+            spot = (0, 0, block, pl.ds(part, 1), slice(None))
+            out[spot] = value
 
 
 def in_smem():
@@ -306,10 +315,13 @@
     layers = w_steps.shape[2]
     f32, bf16 = jnp.float32, jnp.bfloat16
 
-    def exchange(value, flip):
-        pairs = [(i, i ^ flip) for i in range(num_cols * num_rows)]
+    def exchange(value, flip, other_flip):
+        pairs = [
+            (i, i ^ (flip if i % 2 else other_flip)) for i in range(num_cols * num_rows)
+        ]
         return lax.ppermute(value, ("fx", "fy"), pairs)
 
+    near_flip = 2 * num_rows
     arguments = (
         sky_image, vis_coords, col_off, row_off, w_steps, block_codes
     )
@@ -334,9 +346,10 @@
     col_off, row_off, w_steps, block_codes = (
         pltpu.with_memory_space_constraint(value, pltpu.SMEM) for value in scalars
     )
-    pieces = [own_sky]
+    chip_sky = jnp.stack([own_sky, exchange(own_sky, 1, 1)])
+    pieces = [chip_sky]
     for slot in range(1, half_z):
-        pieces.append(exchange(own_sky, 2 * slot * num_rows))
+        pieces.append(exchange(chip_sky, 2 * slot * num_rows, near_flip))
 
     first, twiddle, second = pl.pallas_call(
         functools.partial(
@@ -357,7 +370,6 @@
     limits = jnp.where(
         lax.broadcasted_iota(jnp.int32, (1, LANES), 1) == 0, layer_counts, live_blocks
     )
-    taps = 2 * total_rows
     *tables, planes = pl.pallas_call(
         functools.partial(
             vis_tables_kernel,
@@ -374,7 +386,6 @@
         ),
         name="vis_tables",
         out_shape=(
-            pltpu.VMEM((2 * rows_grid, taps), bf16),
             pltpu.VMEM((2, layers, SG), f32),
             pltpu.VMEM((blocks, 2 * LANES, 2 * vis_count), bf16),
             pltpu.VMEM((blocks, 2, wide, vis_count), f32),
@@ -382,12 +393,16 @@
             pltpu.SMEM((blocks,), jnp.int32),
         ),
         in_specs=[in_smem()] * 3 + [in_vmem()] * 2,
-        out_specs=(in_vmem(),) * 5 + (in_smem(),),
-        scratch_shapes=[pltpu.SMEM((1, LANES), jnp.int32), pltpu.SemaphoreType.DMA],
+        out_specs=(in_vmem(),) * 4 + (in_smem(),),
+        scratch_shapes=[
+            pltpu.SMEM((1, LANES), jnp.int32),
+            pltpu.VMEM((2 * rows_grid, blocks * vis_count), bf16),
+            pltpu.SemaphoreType.DMA,
+        ],
         compiler_params=LIMIT,
     )(row_off, w_steps, block_codes, kept(limits), coords)
 
-    band_shape = pltpu.VMEM((rows_here, 2 * wide, LANES), bf16)
+    band_shape = pltpu.VMEM((2, rows_here, 2 * wide, LANES), bf16)
     own_band, other_band = pl.pallas_call(
         functools.partial(band_kernel, (half_z, facet_rows, fine_cols, rows_here)),
         name="bands",
@@ -400,32 +415,28 @@
     near, far = [own_band], []
     for slot in range(half_y):
         if slot:
-            near.append(exchange(own_band, 2 * slot))
-        far.append(exchange(other_band, num_rows + 2 * slot))
+            near.append(exchange(own_band, 2 * slot, near_flip))
+        far.append(exchange(other_band, num_rows + 2 * slot, near_flip))
     near, far, tables = lax.optimization_barrier((near, far, tables))
     strips = [
         (one.astype(f32) + two.astype(f32)).astype(bf16) for one, two in zip(near, far)
     ]
     own_strips = jnp.stack(strips)
-    other_strips = exchange(own_strips, 1)
-
+    passed_strips = exchange(own_strips, 1, 1)
+
+    operands = [kept(value) for value in (own_strips, passed_strips, *tables)]
     return pl.pallas_call(
-        functools.partial(
-            degrid_kernel, (half_y, rows_here, rows_grid, SG, blocks, layers)
-        ),
+        functools.partial(degrid_kernel, (total_rows, SG, blocks, layers)),
         name="degrid",
         out_shape=jax.ShapeDtypeStruct(vis_coords.shape, f32),
-        in_specs=[in_smem()] + [in_vmem()] * 7,
+        in_specs=[in_smem()] + [in_vmem()] * len(operands),
         out_specs=in_vmem(),
         scratch_shapes=[
-            pltpu.VMEM((2 * half_y * rows_here * 2 * wide, LANES), f32),
-            pltpu.VMEM((layers, wide * rows_grid, 2 * LANES), bf16),
+            pltpu.VMEM((total_rows * 2 * wide, LANES), f32),
+            pltpu.VMEM((layers, wide * total_rows, 2 * LANES), bf16),
         ],
         compiler_params=LIMIT,
-    )(
-        pltpu.with_memory_space_constraint(planes, pltpu.SMEM),
-        *(kept(value) for value in (own_strips, other_strips, *tables)),
-    )
+    )(pltpu.with_memory_space_constraint(planes, pltpu.SMEM), *operands)
 
 
 def solution(mesh):

time: 20.8 us -> 19.3 us (0.928)
  waiting for transfers between devices: 5.49 us -> 3.17 us
  starting transfers between devices: 9.37 us -> 9.85 us
  Pallas kernels: 4.34 us -> 4.65 us
    ppermute x7 -> x8, waiting for transfers between devices: 5.49 us -> 3.17 us  [exchange(): return lax.ppermute(value, ('fx', 'fy'), pairs)]
    ppermute x7 -> x8, starting transfers between devices: 9.37 us -> 9.85 us  [exchange(): return lax.ppermute(value, ('fx', 'fy'), pairs)]
    pallas_call x1, Pallas kernels: 0.43 us -> 0.71 us  [per_device(): pl.pallas_call(functools.partial(band_kernel, (half_z, facet_rows, fine_c...]
  transfers between devices with their start and end apart: 7 -> 8, of which waited for: 3 -> 5; matrix products, arithmetic and copies ran while one was open for 0% -> 0% of each run, Pallas kernels for 8% -> 9%
where the time goes in v2:
time: 19.3 us; the launch traced here: 19.1 us
  starting transfers between devices  9.85 us (51%)
  Pallas kernels  4.65 us (24%)
  waiting for transfers between devices  3.17 us (16%)
  between operations  1.35 us (7%)
    ppermute x8, starting transfers between devices, exchange(): return lax.ppermute(value, ('fx', 'fy'), pairs)  9.85 us
    ppermute x8, waiting for transfers between devices, exchange(): return lax.ppermute(value, ('fx', 'fy'), pairs)  3.17 us
    pallas_call x1, Pallas kernels, per_device(): pl.pallas_call(functools.partial(vis_tables_kernel, (half_y, rows_here, n...  1.52 us
    pallas_call x1, Pallas kernels, per_device(): pl.pallas_call(functools.partial(degrid_kernel, (total_rows, SG, blocks,...  1.3 us
    pallas_call x1, Pallas kernels, per_device(): pl.pallas_call(load_kernel, name='load', out_shape=(pltpu.VMEM((rows_here...  0.87 us
    pallas_call x1, Pallas kernels, per_device(): pl.pallas_call(functools.partial(band_kernel, (half_z, facet_rows, fine_c...  0.71 us
  transfers between devices with their start and end apart: 8, of which 5 were waited for; matrix products, arithmetic and copies ran while one was open for 0% of the time, Pallas kernels for 9%

profile of v2, /device:TPU:0, one launch (start us, length us, event | category | flops | bytes accessed | tf_op | source)
XLA Modules:
  0.0 19.1 jit_solution(13081724683240969848)
XLA Ops:
  0.0 0.9 %load.1 = (bf16[4,16,128]{2,1,0:T(8,128)(2,1)S(1)}, f32[1,1,16,2,128]{4,3,2,1,0:T(2,128)S(1)}, s32[8]{0:T(128)S(4)}, s32[4]{0:T(128)S(4)}, s32[1,1,8]{2,1,0:T(1,128)S(4)}, /*index=5*/s32[1,1,16]{2,1,0:T(1,128)S(4)}) custom-call(f32[4,2048]{1,0:T(4,128)} %refs_0_.1, f32[1,1,16,2,128]{4,3,2,1,0:T(2,128)} %refs_1_.1, s32[8]{0:T(128)} %refs_2_.1, s32[4]{0:T(128)} %refs_3_.1, ...), custom_call_target="tpu_custom_call" | custom-call | tf_op jit(solution)/shard_map/load/pallas_call | solution.py:328
  0.9 0.6 %collective-permute-start = (bf16[4,16,128]{2,1,0:T(8,128)(2,1)S(1)}, bf16[4,16,128]{2,1,0:T(8,128)(2,1)S(1)}, u32[]{:S(2)}, u32[]{:S(2)}) collective-permute-start(bf16[4,16,128]{2,1,0:T(8,128)(2,1)S(1)} %get-tuple-element.34), channel_id=1, source_target_pairs={{0,1},{1,0},{2,3},{3,2},{4,5},{5,4},{6,7},{7,6},{8,9},{9,8},{10,11... | collective-permute-start | bytes 49160 | tf_op jit(solution)/shard_map/ppermute | solution.py:322
  1.4 0.8 %collective-permute-done = bf16[4,16,128]{2,1,0:T(8,128)(2,1)S(1)} collective-permute-done((bf16[4,16,128]{2,1,0:T(8,128)(2,1)S(1)}, bf16[4,16,128]{2,1,0:T(8,128)(2,1)S(1)}, u32[]{:S(2)}, u32[]{:S(2)}) %collective-permute-start) | collective-permute-done | bytes 16416 | tf_op jit(solution)/shard_map/ppermute | solution.py:322
  2.3 2.9 %collective-permute-start.3 = (bf16[2,4,16,128]{3,2,1,0:T(8,128)(2,1)S(1)}, bf16[2,4,16,128]{3,2,1,0:T(8,128)(2,1)S(1)}, u32[]{:S(2)}, u32[]{:S(2)}) collective-permute-start(bf16[2,4,16,128]{3,2,1,0:T(8,128)(2,1)S(1)} %pad_maximum_fusion.1.refs_0_), channel_id=1, source_target_pairs={{0,8},{1,25},{2,10},{3,27},{4,12},{5,29},{6,14},{7,31},{8,0},{9,17... | collective-permute-start | bytes 98312 | tf_op jit(solution)/shard_map/ppermute | solution.py:322
  5.2 0.1 collective-permute-start.2
  5.3 2.0 %collective-permute-start.1 = (bf16[2,4,16,128]{3,2,1,0:T(8,128)(2,1)S(1)}, bf16[2,4,16,128]{3,2,1,0:T(8,128)(2,1)S(1)}, u32[]{:S(2)}, u32[]{:S(2)}) collective-permute-start(bf16[2,4,16,128]{3,2,1,0:T(8,128)(2,1)S(1)} %pad_maximum_fusion.1.refs_0_), channel_id=1, source_target_pairs={{0,8},{1,9},{2,10},{3,11},{4,12},{5,13},{6,14},{7,15},{8,0},{9,1},... | collective-permute-start | bytes 98312 | tf_op jit(solution)/shard_map/ppermute | solution.py:322
  8.5 0.2 %column_tables.1 = (bf16[64,512]{1,0:T(8,128)(2,1)S(1)}, f32[2,128,256]{2,1,0:T(8,128)S(1)}, bf16[16,256]{1,0:T(8,128)(2,1)S(1)}) custom-call(s32[8]{0:T(128)S(4)} %get-tuple-element.35.col_off), custom_call_target="tpu_custom_call" | custom-call | tf_op jit(solution)/shard_map/column_tables/pallas_call | solution.py:354
  8.8 0.0 collective-permute-done.3.refs_3_
  8.8 0.3 %collective-permute-done.2.refs_2_ = bf16[2,4,16,128]{3,2,1,0:T(8,128)(2,1)S(1)} collective-permute-done((bf16[2,4,16,128]{3,2,1,0:T(8,128)(2,1)S(1)}, bf16[2,4,16,128]{3,2,1,0:T(8,128)(2,1)S(1)}, u32[]{:S(2)}, u32[]{:S(2)}) %collective-permute-start.2) | collective-permute-done | bytes 32800 | tf_op jit(solution)/shard_map/ppermute | solution.py:322
  9.1 0.4 %collective-permute-done.1.refs_1_ = bf16[2,4,16,128]{3,2,1,0:T(8,128)(2,1)S(1)} collective-permute-done((bf16[2,4,16,128]{3,2,1,0:T(8,128)(2,1)S(1)}, bf16[2,4,16,128]{3,2,1,0:T(8,128)(2,1)S(1)}, u32[]{:S(2)}, u32[]{:S(2)}) %collective-permute-start.1) | collective-permute-done | bytes 32800 | tf_op jit(solution)/shard_map/ppermute | solution.py:322
  9.5 0.7 %bands.1 = (bf16[2,4,16,128]{3,2,1,0:T(8,128)(2,1)S(1)}, bf16[2,4,16,128]{3,2,1,0:T(8,128)(2,1)S(1)}) custom-call(bf16[2,4,16,128]{3,2,1,0:T(8,128)(2,1)S(1)} %pad_maximum_fusion.1.refs_0_, bf16[2,4,16,128]{3,2,1,0:T(8,128)(2,1)S(1)} %collective-permute-done.1.refs_1_, bf16[2,4,16,128]{3,2,1,0:T(8,128)(2,1)S(1)} %collective-permute-done.2.refs_2_, ...), custom_call_target="tpu_custom_call" | custom-call | tf_op jit(solution)/shard_map/bands/pallas_call | solution.py:406
  10.2 2.0 %collective-permute-start.6 = (bf16[2,4,16,128]{3,2,1,0:T(8,128)(2,1)S(1)}, bf16[2,4,16,128]{3,2,1,0:T(8,128)(2,1)S(1)}, u32[]{:S(2)}, u32[]{:S(2)}) collective-permute-start(bf16[2,4,16,128]{3,2,1,0:T(8,128)(2,1)S(1)} %get-tuple-element.40), channel_id=1, source_target_pairs={{0,8},{1,7},{2,10},{3,5},{4,12},{5,3},{6,14},{7,1},{8,0},{9,15},{1... | collective-permute-start | bytes 98312 | tf_op jit(solution)/shard_map/ppermute | solution.py:322
  12.1 0.1 collective-permute-start.5
  12.2 1.9 %collective-permute-start.4 = (bf16[2,4,16,128]{3,2,1,0:T(8,128)(2,1)S(1)}, bf16[2,4,16,128]{3,2,1,0:T(8,128)(2,1)S(1)}, u32[]{:S(2)}, u32[]{:S(2)}) collective-permute-start(bf16[2,4,16,128]{3,2,1,0:T(8,128)(2,1)S(1)} %get-tuple-element.45), channel_id=1, source_target_pairs={{0,8},{1,3},{2,10},{3,1},{4,12},{5,7},{6,14},{7,5},{8,0},{9,11},{1... | collective-permute-start | bytes 98312 | tf_op jit(solution)/shard_map/ppermute | solution.py:322
  14.2 1.5 %vis_tables.1 = (f32[2,8,1024]{2,1,0:T(8,128)S(1)}, bf16[16,256,256]{2,1,0:T(8,128)(2,1)S(1)}, f32[16,2,8,128]{3,2,1,0:T(8,128)S(1)}, f32[16,2,16,128]{3,2,1,0:T(8,128)S(1)}, s32[16]{0:T(128)S(4)}) custom-call(s32[4]{0:T(128)S(4)} %get-tuple-element.29.row_off, s32[1,1,8]{2,1,0:T(1,128)S(4)} %get-tuple-element.30.steps, ...), custom_call_target="tpu_custom_call" | custom-call | tf_op jit(solution)/shard_map/vis_tables/pallas_call | solution.py:373
  15.7 0.7 %collective-permute-done.4 = bf16[2,4,16,128]{3,2,1,0:T(8,128)(2,1)S(1)} collective-permute-done((bf16[2,4,16,128]{3,2,1,0:T(8,128)(2,1)S(1)}, bf16[2,4,16,128]{3,2,1,0:T(8,128)(2,1)S(1)}, u32[]{:S(2)}, u32[]{:S(2)}) %collective-permute-start.4) | collective-permute-done | bytes 32800 | tf_op jit(solution)/shard_map/ppermute | solution.py:322
  16.4 0.0 collective-permute-done.6
  16.4 0.0 collective-permute-done.5
  16.4 0.4 %collective-permute-start.7 = (bf16[2,2,4,16,128]{4,3,2,1,0:T(8,128)(2,1)S(1)}, bf16[2,2,4,16,128]{4,3,2,1,0:T(8,128)(2,1)S(1)}, u32[]{:S(2)}, u32[]{:S(2)}) collective-permute-start(bf16[2,2,4,16,128]{4,3,2,1,0:T(8,128)(2,1)S(1)} %pad_maximum_fusion.local), channel_id=1, source_target_pairs={{0,1},{1,0},{2,3},{3,2},{4,5},{5,4},{6,7},{7,6},{8,9},{9,8},{10,11... | collective-permute-start | bytes 196616 | tf_op jit(solution)/shard_map/ppermute | solution.py:322
  16.8 0.9 %collective-permute-done.7.passed = bf16[2,2,4,16,128]{4,3,2,1,0:T(8,128)(2,1)S(1)} collective-permute-done((bf16[2,2,4,16,128]{4,3,2,1,0:T(8,128)(2,1)S(1)}, bf16[2,2,4,16,128]{4,3,2,1,0:T(8,128)(2,1)S(1)}, u32[]{:S(2)}, u32[]{:S(2)}) %collective-permute-start.7) | collective-permute-done | bytes 65568 | tf_op jit(solution)/shard_map/ppermute | solution.py:322
  17.8 1.3 %degrid.1 = f32[1,1,16,2,128]{4,3,2,1,0:T(2,128)} custom-call(s32[16]{0:T(128)S(4)} %get-tuple-element.33.planes, bf16[2,2,4,16,128]{4,3,2,1,0:T(8,128)(2,1)S(1)} %pad_maximum_fusion.local, bf16[2,2,4,16,128]{4,3,2,1,0:T(8,128)(2,1)S(1)} %collective-permute-done.7.passed, f32[2,8,1024]{2,1,0:T(8,128)S(1)} %get-tuple-element.49.cols_tab, ...), custom_call_target="tpu_custom_call" | custom-call | tf_op jit(solution)/shard_map/degrid/pallas_call | solution.py:428
  (4 shorter events, 0.0 us)
Async XLA Ops:
  0.9 1.4 %collective-permute-start = (bf16[4,16,128]{2,1,0:T(8,128)(2,1)S(1)}, bf16[4,16,128]{2,1,0:T(8,128)(2,1)S(1)}, u32[]{:S(2)}, u32[]{:S(2)}) collective-permute-start(bf16[4,16,128]{2,1,0:T(8,128)(2,1)S(1)} %get-tuple-element.34), channel_id=1, source_target_pairs={{0,1},{1,0},{2,3},{3,2},{4,5},{5,4},{6,7},{7,6},{8,9},{9,8},{10,11... | collective-permute-start | bytes 49160 | tf_op jit(solution)/shard_map/ppermute | solution.py:322
  2.3 6.5 %collective-permute-start.3 = (bf16[2,4,16,128]{3,2,1,0:T(8,128)(2,1)S(1)}, bf16[2,4,16,128]{3,2,1,0:T(8,128)(2,1)S(1)}, u32[]{:S(2)}, u32[]{:S(2)}) collective-permute-start(bf16[2,4,16,128]{3,2,1,0:T(8,128)(2,1)S(1)} %pad_maximum_fusion.1.refs_0_), channel_id=1, source_target_pairs={{0,8},{1,25},{2,10},{3,27},{4,12},{5,29},{6,14},{7,31},{8,0},{9,17... | collective-permute-start | bytes 98312 | tf_op jit(solution)/shard_map/ppermute | solution.py:322
  5.2 3.9 %collective-permute-start.2 = (bf16[2,4,16,128]{3,2,1,0:T(8,128)(2,1)S(1)}, bf16[2,4,16,128]{3,2,1,0:T(8,128)(2,1)S(1)}, u32[]{:S(2)}, u32[]{:S(2)}) collective-permute-start(bf16[2,4,16,128]{3,2,1,0:T(8,128)(2,1)S(1)} %pad_maximum_fusion.1.refs_0_), channel_id=1, source_target_pairs={{0,8},{1,17},{2,10},{3,19},{4,12},{5,21},{6,14},{7,23},{8,0},{9,25... | collective-permute-start | bytes 98312 | tf_op jit(solution)/shard_map/ppermute | solution.py:322
  5.3 4.2 %collective-permute-start.1 = (bf16[2,4,16,128]{3,2,1,0:T(8,128)(2,1)S(1)}, bf16[2,4,16,128]{3,2,1,0:T(8,128)(2,1)S(1)}, u32[]{:S(2)}, u32[]{:S(2)}) collective-permute-start(bf16[2,4,16,128]{3,2,1,0:T(8,128)(2,1)S(1)} %pad_maximum_fusion.1.refs_0_), channel_id=1, source_target_pairs={{0,8},{1,9},{2,10},{3,11},{4,12},{5,13},{6,14},{7,15},{8,0},{9,1},... | collective-permute-start | bytes 98312 | tf_op jit(solution)/shard_map/ppermute | solution.py:322
  10.2 6.2 %collective-permute-start.6 = (bf16[2,4,16,128]{3,2,1,0:T(8,128)(2,1)S(1)}, bf16[2,4,16,128]{3,2,1,0:T(8,128)(2,1)S(1)}, u32[]{:S(2)}, u32[]{:S(2)}) collective-permute-start(bf16[2,4,16,128]{3,2,1,0:T(8,128)(2,1)S(1)} %get-tuple-element.40), channel_id=1, source_target_pairs={{0,8},{1,7},{2,10},{3,5},{4,12},{5,3},{6,14},{7,1},{8,0},{9,15},{1... | collective-permute-start | bytes 98312 | tf_op jit(solution)/shard_map/ppermute | solution.py:322
  12.1 4.3 %collective-permute-start.5 = (bf16[2,4,16,128]{3,2,1,0:T(8,128)(2,1)S(1)}, bf16[2,4,16,128]{3,2,1,0:T(8,128)(2,1)S(1)}, u32[]{:S(2)}, u32[]{:S(2)}) collective-permute-start(bf16[2,4,16,128]{3,2,1,0:T(8,128)(2,1)S(1)} %get-tuple-element.40), channel_id=1, source_target_pairs={{0,8},{1,5},{2,10},{3,7},{4,12},{5,1},{6,14},{7,3},{8,0},{9,13},{1... | collective-permute-start | bytes 98312 | tf_op jit(solution)/shard_map/ppermute | solution.py:322
  12.2 4.2 %collective-permute-start.4 = (bf16[2,4,16,128]{3,2,1,0:T(8,128)(2,1)S(1)}, bf16[2,4,16,128]{3,2,1,0:T(8,128)(2,1)S(1)}, u32[]{:S(2)}, u32[]{:S(2)}) collective-permute-start(bf16[2,4,16,128]{3,2,1,0:T(8,128)(2,1)S(1)} %get-tuple-element.45), channel_id=1, source_target_pairs={{0,8},{1,3},{2,10},{3,1},{4,12},{5,7},{6,14},{7,5},{8,0},{9,11},{1... | collective-permute-start | bytes 98312 | tf_op jit(solution)/shard_map/ppermute | solution.py:322
  16.4 1.3 %collective-permute-start.7 = (bf16[2,2,4,16,128]{4,3,2,1,0:T(8,128)(2,1)S(1)}, bf16[2,2,4,16,128]{4,3,2,1,0:T(8,128)(2,1)S(1)}, u32[]{:S(2)}, u32[]{:S(2)}) collective-permute-start(bf16[2,2,4,16,128]{4,3,2,1,0:T(8,128)(2,1)S(1)} %pad_maximum_fusion.local), channel_id=1, source_target_pairs={{0,1},{1,0},{2,3},{3,2},{4,5},{5,4},{6,7},{7,6},{8,9},{9,8},{10,11... | collective-permute-start | bytes 196616 | tf_op jit(solution)/shard_map/ppermute | solution.py:322

commit v3 on v2

--- a/solution.py
+++ b/solution.py
@@ -59,6 +59,25 @@
     return lax.broadcasted_iota(jnp.int32, shape, axis)
 
 
+def settle(flat, split, target):
+    rows, pieces, width = target.shape
+    parts = width // LANES
+    for piece in range(pieces):
+        for part in range(parts):
+            split[pl.ds(part * rows * pieces + piece, rows, stride=pieces), :] = flat[
+                :, pl.ds((piece * parts + part) * LANES, LANES)
+            ]
+    for row in range(rows):
+        for part in range(parts):
+            here = pl.ds((part * rows + row) * pieces, pieces)
+            target[row, :, pl.ds(part * LANES, LANES)] = split[here, :].astype(jnp.bfloat16)
+
+
+def pack_kernel(own, passed, out, split):
+    out[0] = own[...]
+    settle(passed, split, out.at[1])
+
+
 def load_kernel(*refs):
     count = (len(refs) - 3) // 2
     sources, (sky_out, *targets) = refs[:count], refs[count : 2 * count]
@@ -70,17 +89,7 @@
     for copy in copies:
         copy.start()
     copies[0].wait()
-    rows, pieces, width = sky_out.shape
-    parts = width // LANES
-    for piece in range(pieces):
-        for part in range(parts):
-            split[pl.ds(part * rows * pieces + piece, rows, stride=pieces), :] = landed[
-                :, pl.ds((piece * parts + part) * LANES, LANES)
-            ]
-    for row in range(rows):
-        for part in range(parts):
-            here = pl.ds((part * rows + row) * pieces, pieces)
-            sky_out[row, :, pl.ds(part * LANES, LANES)] = split[here, :].astype(jnp.bfloat16)
+    settle(landed, split, sky_out)
     for copy in copies[1:]:
         copy.wait()
 
@@ -322,6 +331,7 @@
         return lax.ppermute(value, ("fx", "fy"), pairs)
 
     near_flip = 2 * num_rows
+    passed_sky = exchange(sky_image, 1, 1)
     arguments = (
         sky_image, vis_coords, col_off, row_off, w_steps, block_codes
     )
@@ -346,7 +356,15 @@
     col_off, row_off, w_steps, block_codes = (
         pltpu.with_memory_space_constraint(value, pltpu.SMEM) for value in scalars
     )
-    chip_sky = jnp.stack([own_sky, exchange(own_sky, 1, 1)])
+    chip_sky = pl.pallas_call(
+        pack_kernel,
+        name="pack",
+        out_shape=pltpu.VMEM((2, rows_here, facet_rows, fine_cols), bf16),
+        in_specs=[in_vmem()] * 2,
+        out_specs=in_vmem(),
+        scratch_shapes=[pltpu.VMEM((rows_here * facet_cols // LANES, LANES), f32)],
+        compiler_params=LIMIT,
+    )(kept(own_sky), kept(passed_sky))
     pieces = [chip_sky]
     for slot in range(1, half_z):
         pieces.append(exchange(chip_sky, 2 * slot * num_rows, near_flip))

time: 19.3 us -> 18.6 us (0.964)
  waiting for transfers between devices: 3.17 us -> 2.52 us
    ppermute x8, waiting for transfers between devices: 3.17 us -> 2.52 us  [exchange(): return lax.ppermute(value, ('fx', 'fy'), pairs)]
  transfers between devices with their start and end apart: 8 -> 8, of which waited for: 5 -> 5; matrix products, arithmetic and copies ran while one was open for 0% -> 0% of each run, Pallas kernels for 9% -> 14%
where the time goes in v3:
time: 18.6 us; the launch traced here: 18.4 us
  starting transfers between devices  9.85 us (53%)
  Pallas kernels  4.67 us (25%)
  waiting for transfers between devices  2.52 us (14%)
  between operations  1.35 us (7%)
    ppermute x8, starting transfers between devices, exchange(): return lax.ppermute(value, ('fx', 'fy'), pairs)  9.85 us
    ppermute x8, waiting for transfers between devices, exchange(): return lax.ppermute(value, ('fx', 'fy'), pairs)  2.52 us
    pallas_call x1, Pallas kernels, per_device(): pl.pallas_call(functools.partial(vis_tables_kernel, (half_y, rows_here, n...  1.52 us
    pallas_call x1, Pallas kernels, per_device(): pl.pallas_call(functools.partial(degrid_kernel, (total_rows, SG, blocks,...  1.3 us
    pallas_call x1, Pallas kernels, per_device(): pl.pallas_call(load_kernel, name='load', out_shape=(pltpu.VMEM((rows_here...  0.87 us
    pallas_call x1, Pallas kernels, per_device(): pl.pallas_call(functools.partial(band_kernel, (half_z, facet_rows, fine_c...  0.71 us
  transfers between devices with their start and end apart: 8, of which 5 were waited for; matrix products, arithmetic and copies ran while one was open for 0% of the time, Pallas kernels for 14%

profile of v3, /device:TPU:0, one launch (start us, length us, event | category | flops | bytes accessed | tf_op | source)
XLA Modules:
  0.0 18.4 jit_solution(1864774261747320149)
XLA Ops:
  0.0 0.5 %collective-permute-start = (f32[4,2048]{1,0:T(4,128)}, f32[4,2048]{1,0:T(4,128)S(1)}, u32[]{:S(2)}, u32[]{:S(2)}) collective-permute-start(f32[4,2048]{1,0:T(4,128)} %refs_0_.1), channel_id=1, source_target_pairs={{0,1},{1,0},{2,3},{3,2},{4,5},{5,4},{6,7},{7,6},{8,9},{9,8},{10,11... | collective-permute-start | bytes 98312 | tf_op jit(solution)/shard_map/ppermute | solution.py:331
  0.5 0.9 %load.1 = (bf16[4,16,128]{2,1,0:T(8,128)(2,1)S(1)}, f32[1,1,16,2,128]{4,3,2,1,0:T(2,128)S(1)}, s32[8]{0:T(128)S(4)}, s32[4]{0:T(128)S(4)}, s32[1,1,8]{2,1,0:T(1,128)S(4)}, /*index=5*/s32[1,1,16]{2,1,0:T(1,128)S(4)}) custom-call(f32[4,2048]{1,0:T(4,128)} %refs_0_.1, f32[1,1,16,2,128]{4,3,2,1,0:T(2,128)} %refs_1_.1, s32[8]{0:T(128)} %refs_2_.1, s32[4]{0:T(128)} %refs_3_.1, ...), custom_call_target="tpu_custom_call" | custom-call | tf_op jit(solution)/shard_map/load/pallas_call | solution.py:338
  1.4 0.2 %collective-permute-done.passed = f32[4,2048]{1,0:T(4,128)S(1)} collective-permute-done((f32[4,2048]{1,0:T(4,128)}, f32[4,2048]{1,0:T(4,128)S(1)}, u32[]{:S(2)}, u32[]{:S(2)}) %collective-permute-start) | collective-permute-done | bytes 32800 | tf_op jit(solution)/shard_map/ppermute | solution.py:331
  1.6 3.0 %collective-permute-start.3 = (bf16[2,4,16,128]{3,2,1,0:T(8,128)(2,1)S(1)}, bf16[2,4,16,128]{3,2,1,0:T(8,128)(2,1)S(1)}, u32[]{:S(2)}, u32[]{:S(2)}) collective-permute-start(bf16[2,4,16,128]{3,2,1,0:T(8,128)(2,1)S(1)} %pack.1.refs_0_), channel_id=1, source_target_pairs={{0,8},{1,25},{2,10},{3,27},{4,12},{5,29},{6,14},{7,31},{8,0},{9,17... | collective-permute-start | bytes 98312 | tf_op jit(solution)/shard_map/ppermute | solution.py:331
  4.6 0.1 collective-permute-start.2
  4.6 1.9 %collective-permute-start.1 = (bf16[2,4,16,128]{3,2,1,0:T(8,128)(2,1)S(1)}, bf16[2,4,16,128]{3,2,1,0:T(8,128)(2,1)S(1)}, u32[]{:S(2)}, u32[]{:S(2)}) collective-permute-start(bf16[2,4,16,128]{3,2,1,0:T(8,128)(2,1)S(1)} %pack.1.refs_0_), channel_id=1, source_target_pairs={{0,8},{1,9},{2,10},{3,11},{4,12},{5,13},{6,14},{7,15},{8,0},{9,1},... | collective-permute-start | bytes 98312 | tf_op jit(solution)/shard_map/ppermute | solution.py:331
  7.9 0.2 %column_tables.1 = (bf16[64,512]{1,0:T(8,128)(2,1)S(1)}, f32[2,128,256]{2,1,0:T(8,128)S(1)}, bf16[16,256]{1,0:T(8,128)(2,1)S(1)}) custom-call(s32[8]{0:T(128)S(4)} %get-tuple-element.35.col_off), custom_call_target="tpu_custom_call" | custom-call | tf_op jit(solution)/shard_map/column_tables/pallas_call | solution.py:372
  8.1 0.0 collective-permute-done.3.refs_3_
  8.1 0.3 %collective-permute-done.2.refs_2_ = bf16[2,4,16,128]{3,2,1,0:T(8,128)(2,1)S(1)} collective-permute-done((bf16[2,4,16,128]{3,2,1,0:T(8,128)(2,1)S(1)}, bf16[2,4,16,128]{3,2,1,0:T(8,128)(2,1)S(1)}, u32[]{:S(2)}, u32[]{:S(2)}) %collective-permute-start.2) | collective-permute-done | bytes 32800 | tf_op jit(solution)/shard_map/ppermute | solution.py:331
  8.5 0.4 %collective-permute-done.1.refs_1_ = bf16[2,4,16,128]{3,2,1,0:T(8,128)(2,1)S(1)} collective-permute-done((bf16[2,4,16,128]{3,2,1,0:T(8,128)(2,1)S(1)}, bf16[2,4,16,128]{3,2,1,0:T(8,128)(2,1)S(1)}, u32[]{:S(2)}, u32[]{:S(2)}) %collective-permute-start.1) | collective-permute-done | bytes 32800 | tf_op jit(solution)/shard_map/ppermute | solution.py:331
  8.8 0.7 %bands.1 = (bf16[2,4,16,128]{3,2,1,0:T(8,128)(2,1)S(1)}, bf16[2,4,16,128]{3,2,1,0:T(8,128)(2,1)S(1)}) custom-call(bf16[2,4,16,128]{3,2,1,0:T(8,128)(2,1)S(1)} %pack.1.refs_0_, bf16[2,4,16,128]{3,2,1,0:T(8,128)(2,1)S(1)} %collective-permute-done.1.refs_1_, bf16[2,4,16,128]{3,2,1,0:T(8,128)(2,1)S(1)} %collective-permute-done.2.refs_2_, ...), custom_call_target="tpu_custom_call" | custom-call | tf_op jit(solution)/shard_map/bands/pallas_call | solution.py:424
  9.5 2.0 %collective-permute-start.6 = (bf16[2,4,16,128]{3,2,1,0:T(8,128)(2,1)S(1)}, bf16[2,4,16,128]{3,2,1,0:T(8,128)(2,1)S(1)}, u32[]{:S(2)}, u32[]{:S(2)}) collective-permute-start(bf16[2,4,16,128]{3,2,1,0:T(8,128)(2,1)S(1)} %get-tuple-element.40), channel_id=1, source_target_pairs={{0,8},{1,7},{2,10},{3,5},{4,12},{5,3},{6,14},{7,1},{8,0},{9,15},{1... | collective-permute-start | bytes 98312 | tf_op jit(solution)/shard_map/ppermute | solution.py:331
  11.5 0.1 collective-permute-start.5
  11.6 1.9 %collective-permute-start.4 = (bf16[2,4,16,128]{3,2,1,0:T(8,128)(2,1)S(1)}, bf16[2,4,16,128]{3,2,1,0:T(8,128)(2,1)S(1)}, u32[]{:S(2)}, u32[]{:S(2)}) collective-permute-start(bf16[2,4,16,128]{3,2,1,0:T(8,128)(2,1)S(1)} %get-tuple-element.45), channel_id=1, source_target_pairs={{0,8},{1,3},{2,10},{3,1},{4,12},{5,7},{6,14},{7,5},{8,0},{9,11},{1... | collective-permute-start | bytes 98312 | tf_op jit(solution)/shard_map/ppermute | solution.py:331
  13.5 1.5 %vis_tables.1 = (f32[2,8,1024]{2,1,0:T(8,128)S(1)}, bf16[16,256,256]{2,1,0:T(8,128)(2,1)S(1)}, f32[16,2,8,128]{3,2,1,0:T(8,128)S(1)}, f32[16,2,16,128]{3,2,1,0:T(8,128)S(1)}, s32[16]{0:T(128)S(4)}) custom-call(s32[4]{0:T(128)S(4)} %get-tuple-element.29.row_off, s32[1,1,8]{2,1,0:T(1,128)S(4)} %get-tuple-element.30.steps, ...), custom_call_target="tpu_custom_call" | custom-call | tf_op jit(solution)/shard_map/vis_tables/pallas_call | solution.py:391
  15.1 0.7 %collective-permute-done.4 = bf16[2,4,16,128]{3,2,1,0:T(8,128)(2,1)S(1)} collective-permute-done((bf16[2,4,16,128]{3,2,1,0:T(8,128)(2,1)S(1)}, bf16[2,4,16,128]{3,2,1,0:T(8,128)(2,1)S(1)}, u32[]{:S(2)}, u32[]{:S(2)}) %collective-permute-start.4) | collective-permute-done | bytes 32800 | tf_op jit(solution)/shard_map/ppermute | solution.py:331
  15.8 0.0 collective-permute-done.6
  15.8 0.0 collective-permute-done.5
  15.8 0.4 %collective-permute-start.7 = (bf16[2,2,4,16,128]{4,3,2,1,0:T(8,128)(2,1)S(1)}, bf16[2,2,4,16,128]{4,3,2,1,0:T(8,128)(2,1)S(1)}, u32[]{:S(2)}, u32[]{:S(2)}) collective-permute-start(bf16[2,2,4,16,128]{4,3,2,1,0:T(8,128)(2,1)S(1)} %pad_maximum_fusion.local), channel_id=1, source_target_pairs={{0,1},{1,0},{2,3},{3,2},{4,5},{5,4},{6,7},{7,6},{8,9},{9,8},{10,11... | collective-permute-start | bytes 196616 | tf_op jit(solution)/shard_map/ppermute | solution.py:331
  16.2 0.9 %collective-permute-done.7.passed = bf16[2,2,4,16,128]{4,3,2,1,0:T(8,128)(2,1)S(1)} collective-permute-done((bf16[2,2,4,16,128]{4,3,2,1,0:T(8,128)(2,1)S(1)}, bf16[2,2,4,16,128]{4,3,2,1,0:T(8,128)(2,1)S(1)}, u32[]{:S(2)}, u32[]{:S(2)}) %collective-permute-start.7) | collective-permute-done | bytes 65568 | tf_op jit(solution)/shard_map/ppermute | solution.py:331
  17.1 1.3 %degrid.1 = f32[1,1,16,2,128]{4,3,2,1,0:T(2,128)} custom-call(s32[16]{0:T(128)S(4)} %get-tuple-element.33.planes, bf16[2,2,4,16,128]{4,3,2,1,0:T(8,128)(2,1)S(1)} %pad_maximum_fusion.local, bf16[2,2,4,16,128]{4,3,2,1,0:T(8,128)(2,1)S(1)} %collective-permute-done.7.passed, f32[2,8,1024]{2,1,0:T(8,128)S(1)} %get-tuple-element.49.cols_tab, ...), custom_call_target="tpu_custom_call" | custom-call | tf_op jit(solution)/shard_map/degrid/pallas_call | solution.py:446
  (4 shorter events, 0.1 us)
Async XLA Ops:
  0.0 1.6 %collective-permute-start = (f32[4,2048]{1,0:T(4,128)}, f32[4,2048]{1,0:T(4,128)S(1)}, u32[]{:S(2)}, u32[]{:S(2)}) collective-permute-start(f32[4,2048]{1,0:T(4,128)} %refs_0_.1), channel_id=1, source_target_pairs={{0,1},{1,0},{2,3},{3,2},{4,5},{5,4},{6,7},{7,6},{8,9},{9,8},{10,11... | collective-permute-start | bytes 98312 | tf_op jit(solution)/shard_map/ppermute | solution.py:331
  1.6 6.6 %collective-permute-start.3 = (bf16[2,4,16,128]{3,2,1,0:T(8,128)(2,1)S(1)}, bf16[2,4,16,128]{3,2,1,0:T(8,128)(2,1)S(1)}, u32[]{:S(2)}, u32[]{:S(2)}) collective-permute-start(bf16[2,4,16,128]{3,2,1,0:T(8,128)(2,1)S(1)} %pack.1.refs_0_), channel_id=1, source_target_pairs={{0,8},{1,25},{2,10},{3,27},{4,12},{5,29},{6,14},{7,31},{8,0},{9,17... | collective-permute-start | bytes 98312 | tf_op jit(solution)/shard_map/ppermute | solution.py:331
  4.6 3.9 %collective-permute-start.2 = (bf16[2,4,16,128]{3,2,1,0:T(8,128)(2,1)S(1)}, bf16[2,4,16,128]{3,2,1,0:T(8,128)(2,1)S(1)}, u32[]{:S(2)}, u32[]{:S(2)}) collective-permute-start(bf16[2,4,16,128]{3,2,1,0:T(8,128)(2,1)S(1)} %pack.1.refs_0_), channel_id=1, source_target_pairs={{0,8},{1,17},{2,10},{3,19},{4,12},{5,21},{6,14},{7,23},{8,0},{9,25... | collective-permute-start | bytes 98312 | tf_op jit(solution)/shard_map/ppermute | solution.py:331
  4.6 4.2 %collective-permute-start.1 = (bf16[2,4,16,128]{3,2,1,0:T(8,128)(2,1)S(1)}, bf16[2,4,16,128]{3,2,1,0:T(8,128)(2,1)S(1)}, u32[]{:S(2)}, u32[]{:S(2)}) collective-permute-start(bf16[2,4,16,128]{3,2,1,0:T(8,128)(2,1)S(1)} %pack.1.refs_0_), channel_id=1, source_target_pairs={{0,8},{1,9},{2,10},{3,11},{4,12},{5,13},{6,14},{7,15},{8,0},{9,1},... | collective-permute-start | bytes 98312 | tf_op jit(solution)/shard_map/ppermute | solution.py:331
  9.5 6.2 %collective-permute-start.6 = (bf16[2,4,16,128]{3,2,1,0:T(8,128)(2,1)S(1)}, bf16[2,4,16,128]{3,2,1,0:T(8,128)(2,1)S(1)}, u32[]{:S(2)}, u32[]{:S(2)}) collective-permute-start(bf16[2,4,16,128]{3,2,1,0:T(8,128)(2,1)S(1)} %get-tuple-element.40), channel_id=1, source_target_pairs={{0,8},{1,7},{2,10},{3,5},{4,12},{5,3},{6,14},{7,1},{8,0},{9,15},{1... | collective-permute-start | bytes 98312 | tf_op jit(solution)/shard_map/ppermute | solution.py:331
  11.5 4.3 %collective-permute-start.5 = (bf16[2,4,16,128]{3,2,1,0:T(8,128)(2,1)S(1)}, bf16[2,4,16,128]{3,2,1,0:T(8,128)(2,1)S(1)}, u32[]{:S(2)}, u32[]{:S(2)}) collective-permute-start(bf16[2,4,16,128]{3,2,1,0:T(8,128)(2,1)S(1)} %get-tuple-element.40), channel_id=1, source_target_pairs={{0,8},{1,5},{2,10},{3,7},{4,12},{5,1},{6,14},{7,3},{8,0},{9,13},{1... | collective-permute-start | bytes 98312 | tf_op jit(solution)/shard_map/ppermute | solution.py:331
  11.6 4.2 %collective-permute-start.4 = (bf16[2,4,16,128]{3,2,1,0:T(8,128)(2,1)S(1)}, bf16[2,4,16,128]{3,2,1,0:T(8,128)(2,1)S(1)}, u32[]{:S(2)}, u32[]{:S(2)}) collective-permute-start(bf16[2,4,16,128]{3,2,1,0:T(8,128)(2,1)S(1)} %get-tuple-element.45), channel_id=1, source_target_pairs={{0,8},{1,3},{2,10},{3,1},{4,12},{5,7},{6,14},{7,5},{8,0},{9,11},{1... | collective-permute-start | bytes 98312 | tf_op jit(solution)/shard_map/ppermute | solution.py:331
  15.8 1.3 %collective-permute-start.7 = (bf16[2,2,4,16,128]{4,3,2,1,0:T(8,128)(2,1)S(1)}, bf16[2,2,4,16,128]{4,3,2,1,0:T(8,128)(2,1)S(1)}, u32[]{:S(2)}, u32[]{:S(2)}) collective-permute-start(bf16[2,2,4,16,128]{4,3,2,1,0:T(8,128)(2,1)S(1)} %pad_maximum_fusion.local), channel_id=1, source_target_pairs={{0,1},{1,0},{2,3},{3,2},{4,5},{5,4},{6,7},{7,6},{8,9},{9,8},{10,11... | collective-permute-start | bytes 196616 | tf_op jit(solution)/shard_map/ppermute | solution.py:331

commit v4 on v3

--- a/solution.py
+++ b/solution.py
@@ -97,17 +97,17 @@
 def column_tables_kernel(dims, col_off, first, twiddle, second):
     half_z, facet_rows, fine_cols, total_cols, wide, scale = dims
     here = lax.axis_index("fx")
+    for slot in range(half_z):
+        row = facet_rows * (here ^ (2 * slot)) + iota((facet_rows, LANES), 0)
+        cosine, sine = turn_of_int(row * iota((facet_rows, LANES), 1), LANES)
+        rows = pl.ds(slot * facet_rows, facet_rows)
+        first[rows, pl.ds(0, LANES)] = cosine.astype(jnp.bfloat16)
+        first[rows, pl.ds(LANES, LANES)] = (-sine).astype(jnp.bfloat16)
     for target in range(2):
         offset = col_off[here ^ target]
-        residue = offset + iota((facet_rows, LANES), 1)
-        for slot in range(half_z):
-            row = facet_rows * (here ^ (2 * slot)) + iota((facet_rows, LANES), 0)
-            cosine, sine = turn_of_int(row * residue, LANES)
-            rows = pl.ds(slot * facet_rows, facet_rows)
-            first[rows, pl.ds(target * LANES, LANES)] = cosine.astype(jnp.bfloat16)
-            first[rows, pl.ds((2 + target) * LANES, LANES)] = (-sine).astype(jnp.bfloat16)
-        phase = iota((fine_cols, LANES), 0) * (offset + iota((fine_cols, LANES), 1))
-        cosine, sine = turn_of_int(phase, total_cols)
+        residue = iota((fine_cols, LANES), 1)
+        step = (residue - offset) & (LANES - 1)
+        cosine, sine = turn_of_int(iota((fine_cols, LANES), 0) * (offset + step), total_cols)
         cols = pl.ds(target * LANES, LANES)
         twiddle[0, :, cols] = cosine * scale
         twiddle[1, :, cols] = sine * (-scale)
@@ -118,8 +118,10 @@
     second[pl.ds(wide, wide), pl.ds(fine_cols, fine_cols)] = cosine.astype(jnp.bfloat16)
 
 
-def band_kernel(dims, *refs):
+def band_kernel(dims, col_off, *refs):
     half_z, facet_rows, fine_cols, rows_here = dims
+    here = lax.axis_index("fx")
+    shifts = [(-col_off[here ^ target]) & (LANES - 1) for target in range(2)]
     pieces = refs[:half_z]
     first, twiddle, second, own_out, other_out = refs[half_z:]
     twist_real = twiddle[0]
@@ -137,8 +139,8 @@
         )
         for row in range(rows_here):
             part = spread[row * fine_cols : (row + 1) * fine_cols]
-            part_real = part[:, : 2 * LANES]
-            part_imag = part[:, 2 * LANES :]
+            part_real = jnp.concatenate([part[:, :LANES]] * 2, axis=1)
+            part_imag = jnp.concatenate([part[:, LANES:]] * 2, axis=1)
             turned = jnp.concatenate(
                 [
                     part_real * twist_real - part_imag * twist_imag,
@@ -147,9 +149,9 @@
                 axis=0,
             ).astype(jnp.bfloat16)
             bands = jnp.dot(second[...], turned, preferred_element_type=jnp.float32)
-            bands = bands.astype(jnp.bfloat16)
-            own_out[held, row] = bands[:, :LANES]
-            other_out[held, row] = bands[:, LANES:]
+            for target, out in enumerate((own_out, other_out)):
+                band = bands[:, target * LANES : (target + 1) * LANES]
+                out[held, row] = pltpu.roll(band, shifts[target], 1).astype(jnp.bfloat16)
 
 
 def vis_tables_kernel(
@@ -376,7 +378,7 @@
         ),
         name="column_tables",
         out_shape=(
-            pltpu.VMEM((half_z * facet_rows, 4 * LANES), bf16),
+            pltpu.VMEM((half_z * facet_rows, 2 * LANES), bf16),
             pltpu.VMEM((2, fine_cols, 2 * LANES), f32),
             pltpu.VMEM((2 * wide, 2 * fine_cols), bf16),
         ),
@@ -425,10 +427,10 @@
         functools.partial(band_kernel, (half_z, facet_rows, fine_cols, rows_here)),
         name="bands",
         out_shape=(band_shape, band_shape),
-        in_specs=[in_vmem()] * (half_z + 3),
+        in_specs=[in_smem()] + [in_vmem()] * (half_z + 3),
         out_specs=(in_vmem(),) * 2,
         compiler_params=LIMIT,
-    )(*(kept(value) for value in (*pieces, first, twiddle, second)))
+    )(col_off, *(kept(value) for value in (*pieces, first, twiddle, second)))
 
     near, far = [own_band], []
     for slot in range(half_y):

time: 18.6 us -> 18.5 us (level)
  no operation moved by 1% of the time
where the time goes in v4:
time: 18.5 us; the launch traced here: 18.3 us
  starting transfers between devices  9.84 us (53%)
  Pallas kernels  4.56 us (25%)
  waiting for transfers between devices  2.56 us (14%)
  between operations  1.35 us (7%)
    ppermute x8, starting transfers between devices, exchange(): return lax.ppermute(value, ('fx', 'fy'), pairs)  9.84 us
    ppermute x8, waiting for transfers between devices, exchange(): return lax.ppermute(value, ('fx', 'fy'), pairs)  2.56 us
    pallas_call x1, Pallas kernels, per_device(): pl.pallas_call(functools.partial(vis_tables_kernel, (half_y, rows_here, n...  1.52 us
    pallas_call x1, Pallas kernels, per_device(): pl.pallas_call(functools.partial(degrid_kernel, (total_rows, SG, blocks,...  1.3 us
    pallas_call x1, Pallas kernels, per_device(): pl.pallas_call(load_kernel, name='load', out_shape=(pltpu.VMEM((rows_here...  0.87 us
    pallas_call x1, Pallas kernels, per_device(): pl.pallas_call(functools.partial(band_kernel, (half_z, facet_rows, fine_c...  0.64 us
  transfers between devices with their start and end apart: 8, of which 5 were waited for; matrix products, arithmetic and copies ran while one was open for 0% of the time, Pallas kernels for 14%

profile of v4, /device:TPU:0, one launch (start us, length us, event | category | flops | bytes accessed | tf_op | source)
XLA Modules:
  0.0 18.3 jit_solution(16308528914440098054)
XLA Ops:
  0.0 0.5 %collective-permute-start = (f32[4,2048]{1,0:T(4,128)}, f32[4,2048]{1,0:T(4,128)S(1)}, u32[]{:S(2)}, u32[]{:S(2)}) collective-permute-start(f32[4,2048]{1,0:T(4,128)} %refs_0_.1), channel_id=1, source_target_pairs={{0,1},{1,0},{2,3},{3,2},{4,5},{5,4},{6,7},{7,6},{8,9},{9,8},{10,11... | collective-permute-start | bytes 98312 | tf_op jit(solution)/shard_map/ppermute | solution.py:333
  0.5 0.9 %load.1 = (bf16[4,16,128]{2,1,0:T(8,128)(2,1)S(1)}, f32[1,1,16,2,128]{4,3,2,1,0:T(2,128)S(1)}, s32[8]{0:T(128)S(4)}, s32[4]{0:T(128)S(4)}, s32[1,1,8]{2,1,0:T(1,128)S(4)}, /*index=5*/s32[1,1,16]{2,1,0:T(1,128)S(4)}) custom-call(f32[4,2048]{1,0:T(4,128)} %refs_0_.1, f32[1,1,16,2,128]{4,3,2,1,0:T(2,128)} %refs_1_.1, s32[8]{0:T(128)} %refs_2_.1, s32[4]{0:T(128)} %refs_3_.1, ...), custom_call_target="tpu_custom_call" | custom-call | tf_op jit(solution)/shard_map/load/pallas_call | solution.py:340
  1.4 0.2 %collective-permute-done.passed = f32[4,2048]{1,0:T(4,128)S(1)} collective-permute-done((f32[4,2048]{1,0:T(4,128)}, f32[4,2048]{1,0:T(4,128)S(1)}, u32[]{:S(2)}, u32[]{:S(2)}) %collective-permute-start) | collective-permute-done | bytes 32800 | tf_op jit(solution)/shard_map/ppermute | solution.py:333
  1.6 3.0 %collective-permute-start.3 = (bf16[2,4,16,128]{3,2,1,0:T(8,128)(2,1)S(1)}, bf16[2,4,16,128]{3,2,1,0:T(8,128)(2,1)S(1)}, u32[]{:S(2)}, u32[]{:S(2)}) collective-permute-start(bf16[2,4,16,128]{3,2,1,0:T(8,128)(2,1)S(1)} %pack.1.refs_0_), channel_id=1, source_target_pairs={{0,8},{1,25},{2,10},{3,27},{4,12},{5,29},{6,14},{7,31},{8,0},{9,17... | collective-permute-start | bytes 98312 | tf_op jit(solution)/shard_map/ppermute | solution.py:333
  4.6 0.1 collective-permute-start.2
  4.6 1.9 %collective-permute-start.1 = (bf16[2,4,16,128]{3,2,1,0:T(8,128)(2,1)S(1)}, bf16[2,4,16,128]{3,2,1,0:T(8,128)(2,1)S(1)}, u32[]{:S(2)}, u32[]{:S(2)}) collective-permute-start(bf16[2,4,16,128]{3,2,1,0:T(8,128)(2,1)S(1)} %pack.1.refs_0_), channel_id=1, source_target_pairs={{0,8},{1,9},{2,10},{3,11},{4,12},{5,13},{6,14},{7,15},{8,0},{9,1},... | collective-permute-start | bytes 98312 | tf_op jit(solution)/shard_map/ppermute | solution.py:333
  7.9 0.2 %column_tables.1 = (bf16[64,256]{1,0:T(8,128)(2,1)S(1)}, f32[2,128,256]{2,1,0:T(8,128)S(1)}, bf16[16,256]{1,0:T(8,128)(2,1)S(1)}) custom-call(s32[8]{0:T(128)S(4)} %get-tuple-element.34.col_off), custom_call_target="tpu_custom_call" | custom-call | tf_op jit(solution)/shard_map/column_tables/pallas_call | solution.py:374
  8.1 0.0 collective-permute-done.3.refs_3_
  8.1 0.4 %collective-permute-done.2.refs_2_ = bf16[2,4,16,128]{3,2,1,0:T(8,128)(2,1)S(1)} collective-permute-done((bf16[2,4,16,128]{3,2,1,0:T(8,128)(2,1)S(1)}, bf16[2,4,16,128]{3,2,1,0:T(8,128)(2,1)S(1)}, u32[]{:S(2)}, u32[]{:S(2)}) %collective-permute-start.2) | collective-permute-done | bytes 32800 | tf_op jit(solution)/shard_map/ppermute | solution.py:333
  8.5 0.4 %collective-permute-done.1.refs_1_ = bf16[2,4,16,128]{3,2,1,0:T(8,128)(2,1)S(1)} collective-permute-done((bf16[2,4,16,128]{3,2,1,0:T(8,128)(2,1)S(1)}, bf16[2,4,16,128]{3,2,1,0:T(8,128)(2,1)S(1)}, u32[]{:S(2)}, u32[]{:S(2)}) %collective-permute-start.1) | collective-permute-done | bytes 32800 | tf_op jit(solution)/shard_map/ppermute | solution.py:333
  8.8 0.6 %bands.1 = (bf16[2,4,16,128]{3,2,1,0:T(8,128)(2,1)S(1)}, bf16[2,4,16,128]{3,2,1,0:T(8,128)(2,1)S(1)}) custom-call(s32[8]{0:T(128)S(4)} %get-tuple-element.34.col_off, bf16[2,4,16,128]{3,2,1,0:T(8,128)(2,1)S(1)} %pack.1.refs_0_, bf16[2,4,16,128]{3,2,1,0:T(8,128)(2,1)S(1)} %collective-permute-done.1.refs_1_, ...), custom_call_target="tpu_custom_call" | custom-call | tf_op jit(solution)/shard_map/bands/pallas_call | solution.py:426
  9.5 2.0 %collective-permute-start.6 = (bf16[2,4,16,128]{3,2,1,0:T(8,128)(2,1)S(1)}, bf16[2,4,16,128]{3,2,1,0:T(8,128)(2,1)S(1)}, u32[]{:S(2)}, u32[]{:S(2)}) collective-permute-start(bf16[2,4,16,128]{3,2,1,0:T(8,128)(2,1)S(1)} %get-tuple-element.40), channel_id=1, source_target_pairs={{0,8},{1,7},{2,10},{3,5},{4,12},{5,3},{6,14},{7,1},{8,0},{9,15},{1... | collective-permute-start | bytes 98312 | tf_op jit(solution)/shard_map/ppermute | solution.py:333
  11.4 0.1 collective-permute-start.5
  11.5 1.9 %collective-permute-start.4 = (bf16[2,4,16,128]{3,2,1,0:T(8,128)(2,1)S(1)}, bf16[2,4,16,128]{3,2,1,0:T(8,128)(2,1)S(1)}, u32[]{:S(2)}, u32[]{:S(2)}) collective-permute-start(bf16[2,4,16,128]{3,2,1,0:T(8,128)(2,1)S(1)} %get-tuple-element.45), channel_id=1, source_target_pairs={{0,8},{1,3},{2,10},{3,1},{4,12},{5,7},{6,14},{7,5},{8,0},{9,11},{1... | collective-permute-start | bytes 98312 | tf_op jit(solution)/shard_map/ppermute | solution.py:333
  13.4 1.5 %vis_tables.1 = (f32[2,8,1024]{2,1,0:T(8,128)S(1)}, bf16[16,256,256]{2,1,0:T(8,128)(2,1)S(1)}, f32[16,2,8,128]{3,2,1,0:T(8,128)S(1)}, f32[16,2,16,128]{3,2,1,0:T(8,128)S(1)}, s32[16]{0:T(128)S(4)}) custom-call(s32[4]{0:T(128)S(4)} %get-tuple-element.29.row_off, s32[1,1,8]{2,1,0:T(1,128)S(4)} %get-tuple-element.30.steps, ...), custom_call_target="tpu_custom_call" | custom-call | tf_op jit(solution)/shard_map/vis_tables/pallas_call | solution.py:393
  15.0 0.7 %collective-permute-done.4 = bf16[2,4,16,128]{3,2,1,0:T(8,128)(2,1)S(1)} collective-permute-done((bf16[2,4,16,128]{3,2,1,0:T(8,128)(2,1)S(1)}, bf16[2,4,16,128]{3,2,1,0:T(8,128)(2,1)S(1)}, u32[]{:S(2)}, u32[]{:S(2)}) %collective-permute-start.4) | collective-permute-done | bytes 32800 | tf_op jit(solution)/shard_map/ppermute | solution.py:333
  15.7 0.0 collective-permute-done.6
  15.7 0.0 collective-permute-done.5
  15.7 0.4 %collective-permute-start.7 = (bf16[2,2,4,16,128]{4,3,2,1,0:T(8,128)(2,1)S(1)}, bf16[2,2,4,16,128]{4,3,2,1,0:T(8,128)(2,1)S(1)}, u32[]{:S(2)}, u32[]{:S(2)}) collective-permute-start(bf16[2,2,4,16,128]{4,3,2,1,0:T(8,128)(2,1)S(1)} %pad_maximum_fusion.local), channel_id=1, source_target_pairs={{0,1},{1,0},{2,3},{3,2},{4,5},{5,4},{6,7},{7,6},{8,9},{9,8},{10,11... | collective-permute-start | bytes 196616 | tf_op jit(solution)/shard_map/ppermute | solution.py:333
  16.1 0.9 %collective-permute-done.7.passed = bf16[2,2,4,16,128]{4,3,2,1,0:T(8,128)(2,1)S(1)} collective-permute-done((bf16[2,2,4,16,128]{4,3,2,1,0:T(8,128)(2,1)S(1)}, bf16[2,2,4,16,128]{4,3,2,1,0:T(8,128)(2,1)S(1)}, u32[]{:S(2)}, u32[]{:S(2)}) %collective-permute-start.7) | collective-permute-done | bytes 65568 | tf_op jit(solution)/shard_map/ppermute | solution.py:333
  17.1 1.3 %degrid.1 = f32[1,1,16,2,128]{4,3,2,1,0:T(2,128)} custom-call(s32[16]{0:T(128)S(4)} %get-tuple-element.33.planes, bf16[2,2,4,16,128]{4,3,2,1,0:T(8,128)(2,1)S(1)} %pad_maximum_fusion.local, bf16[2,2,4,16,128]{4,3,2,1,0:T(8,128)(2,1)S(1)} %collective-permute-done.7.passed, f32[2,8,1024]{2,1,0:T(8,128)S(1)} %get-tuple-element.49.cols_tab, ...), custom_call_target="tpu_custom_call" | custom-call | tf_op jit(solution)/shard_map/degrid/pallas_call | solution.py:448
  (4 shorter events, 0.1 us)
Async XLA Ops:
  0.0 1.6 %collective-permute-start = (f32[4,2048]{1,0:T(4,128)}, f32[4,2048]{1,0:T(4,128)S(1)}, u32[]{:S(2)}, u32[]{:S(2)}) collective-permute-start(f32[4,2048]{1,0:T(4,128)} %refs_0_.1), channel_id=1, source_target_pairs={{0,1},{1,0},{2,3},{3,2},{4,5},{5,4},{6,7},{7,6},{8,9},{9,8},{10,11... | collective-permute-start | bytes 98312 | tf_op jit(solution)/shard_map/ppermute | solution.py:333
  1.6 6.5 %collective-permute-start.3 = (bf16[2,4,16,128]{3,2,1,0:T(8,128)(2,1)S(1)}, bf16[2,4,16,128]{3,2,1,0:T(8,128)(2,1)S(1)}, u32[]{:S(2)}, u32[]{:S(2)}) collective-permute-start(bf16[2,4,16,128]{3,2,1,0:T(8,128)(2,1)S(1)} %pack.1.refs_0_), channel_id=1, source_target_pairs={{0,8},{1,25},{2,10},{3,27},{4,12},{5,29},{6,14},{7,31},{8,0},{9,17... | collective-permute-start | bytes 98312 | tf_op jit(solution)/shard_map/ppermute | solution.py:333
  4.6 3.9 %collective-permute-start.2 = (bf16[2,4,16,128]{3,2,1,0:T(8,128)(2,1)S(1)}, bf16[2,4,16,128]{3,2,1,0:T(8,128)(2,1)S(1)}, u32[]{:S(2)}, u32[]{:S(2)}) collective-permute-start(bf16[2,4,16,128]{3,2,1,0:T(8,128)(2,1)S(1)} %pack.1.refs_0_), channel_id=1, source_target_pairs={{0,8},{1,17},{2,10},{3,19},{4,12},{5,21},{6,14},{7,23},{8,0},{9,25... | collective-permute-start | bytes 98312 | tf_op jit(solution)/shard_map/ppermute | solution.py:333
  4.6 4.2 %collective-permute-start.1 = (bf16[2,4,16,128]{3,2,1,0:T(8,128)(2,1)S(1)}, bf16[2,4,16,128]{3,2,1,0:T(8,128)(2,1)S(1)}, u32[]{:S(2)}, u32[]{:S(2)}) collective-permute-start(bf16[2,4,16,128]{3,2,1,0:T(8,128)(2,1)S(1)} %pack.1.refs_0_), channel_id=1, source_target_pairs={{0,8},{1,9},{2,10},{3,11},{4,12},{5,13},{6,14},{7,15},{8,0},{9,1},... | collective-permute-start | bytes 98312 | tf_op jit(solution)/shard_map/ppermute | solution.py:333
  9.5 6.2 %collective-permute-start.6 = (bf16[2,4,16,128]{3,2,1,0:T(8,128)(2,1)S(1)}, bf16[2,4,16,128]{3,2,1,0:T(8,128)(2,1)S(1)}, u32[]{:S(2)}, u32[]{:S(2)}) collective-permute-start(bf16[2,4,16,128]{3,2,1,0:T(8,128)(2,1)S(1)} %get-tuple-element.40), channel_id=1, source_target_pairs={{0,8},{1,7},{2,10},{3,5},{4,12},{5,3},{6,14},{7,1},{8,0},{9,15},{1... | collective-permute-start | bytes 98312 | tf_op jit(solution)/shard_map/ppermute | solution.py:333
  11.4 4.3 %collective-permute-start.5 = (bf16[2,4,16,128]{3,2,1,0:T(8,128)(2,1)S(1)}, bf16[2,4,16,128]{3,2,1,0:T(8,128)(2,1)S(1)}, u32[]{:S(2)}, u32[]{:S(2)}) collective-permute-start(bf16[2,4,16,128]{3,2,1,0:T(8,128)(2,1)S(1)} %get-tuple-element.40), channel_id=1, source_target_pairs={{0,8},{1,5},{2,10},{3,7},{4,12},{5,1},{6,14},{7,3},{8,0},{9,13},{1... | collective-permute-start | bytes 98312 | tf_op jit(solution)/shard_map/ppermute | solution.py:333
  11.5 4.2 %collective-permute-start.4 = (bf16[2,4,16,128]{3,2,1,0:T(8,128)(2,1)S(1)}, bf16[2,4,16,128]{3,2,1,0:T(8,128)(2,1)S(1)}, u32[]{:S(2)}, u32[]{:S(2)}) collective-permute-start(bf16[2,4,16,128]{3,2,1,0:T(8,128)(2,1)S(1)} %get-tuple-element.45), channel_id=1, source_target_pairs={{0,8},{1,3},{2,10},{3,1},{4,12},{5,7},{6,14},{7,5},{8,0},{9,11},{1... | collective-permute-start | bytes 98312 | tf_op jit(solution)/shard_map/ppermute | solution.py:333
  15.7 1.3 %collective-permute-start.7 = (bf16[2,2,4,16,128]{4,3,2,1,0:T(8,128)(2,1)S(1)}, bf16[2,2,4,16,128]{4,3,2,1,0:T(8,128)(2,1)S(1)}, u32[]{:S(2)}, u32[]{:S(2)}) collective-permute-start(bf16[2,2,4,16,128]{4,3,2,1,0:T(8,128)(2,1)S(1)} %pad_maximum_fusion.local), channel_id=1, source_target_pairs={{0,1},{1,0},{2,3},{3,2},{4,5},{5,4},{6,7},{7,6},{8,9},{9,8},{10,11... | collective-permute-start | bytes 196616 | tf_op jit(solution)/shard_map/ppermute | solution.py:333

commit v5 on v4

--- a/solution.py
+++ b/solution.py
@@ -118,11 +118,15 @@
     second[pl.ds(wide, wide), pl.ds(fine_cols, fine_cols)] = cosine.astype(jnp.bfloat16)
 
 
+def slot_order(half_z):
+    return [*range(min(2, half_z)), *range(half_z - 1, 1, -1)]
+
+
 def band_kernel(dims, col_off, *refs):
     half_z, facet_rows, fine_cols, rows_here = dims
     here = lax.axis_index("fx")
     shifts = [(-col_off[here ^ target]) & (LANES - 1) for target in range(2)]
-    pieces = refs[:half_z]
+    pieces = [refs[place] for place in slot_order(half_z)]
     first, twiddle, second, own_out, other_out = refs[half_z:]
     twist_real = twiddle[0]
     twist_imag = twiddle[1]
@@ -371,6 +375,8 @@
     for slot in range(1, half_z):
         pieces.append(exchange(chip_sky, 2 * slot * num_rows, near_flip))
 
+    operands = [pieces[slot] for slot in slot_order(half_z)]
+
     first, twiddle, second = pl.pallas_call(
         functools.partial(
             column_tables_kernel,
@@ -430,7 +436,7 @@
         in_specs=[in_smem()] + [in_vmem()] * (half_z + 3),
         out_specs=(in_vmem(),) * 2,
         compiler_params=LIMIT,
-    )(col_off, *(kept(value) for value in (*pieces, first, twiddle, second)))
+    )(col_off, *(kept(value) for value in (*operands, first, twiddle, second)))
 
     near, far = [own_band], []
     for slot in range(half_y):

time: 18.5 us -> 18.4 us (level)
  no operation moved by 1% of the time
where the time goes in v5:
time: 18.4 us; the launch traced here: 18.2 us
  starting transfers between devices  9.77 us (53%)
  Pallas kernels  4.56 us (25%)
  waiting for transfers between devices  2.53 us (14%)
  between operations  1.35 us (7%)
    ppermute x8, starting transfers between devices, exchange(): return lax.ppermute(value, ('fx', 'fy'), pairs)  9.77 us
    ppermute x8, waiting for transfers between devices, exchange(): return lax.ppermute(value, ('fx', 'fy'), pairs)  2.53 us
    pallas_call x1, Pallas kernels, per_device(): pl.pallas_call(functools.partial(vis_tables_kernel, (half_y, rows_here, n...  1.52 us
    pallas_call x1, Pallas kernels, per_device(): pl.pallas_call(functools.partial(degrid_kernel, (total_rows, SG, blocks,...  1.3 us
    pallas_call x1, Pallas kernels, per_device(): pl.pallas_call(load_kernel, name='load', out_shape=(pltpu.VMEM((rows_here...  0.87 us
    pallas_call x1, Pallas kernels, per_device(): pl.pallas_call(functools.partial(band_kernel, (half_z, facet_rows, fine_c...  0.64 us
  transfers between devices with their start and end apart: 8, of which 5 were waited for; matrix products, arithmetic and copies ran while one was open for 0% of the time, Pallas kernels for 14%

profile of v5, /device:TPU:0, one launch (start us, length us, event | category | flops | bytes accessed | tf_op | source)
XLA Modules:
  0.0 18.2 jit_solution(4419177299732308942)
XLA Ops:
  0.0 0.5 %collective-permute-start = (f32[4,2048]{1,0:T(4,128)}, f32[4,2048]{1,0:T(4,128)S(1)}, u32[]{:S(2)}, u32[]{:S(2)}) collective-permute-start(f32[4,2048]{1,0:T(4,128)} %refs_0_.1), channel_id=1, source_target_pairs={{0,1},{1,0},{2,3},{3,2},{4,5},{5,4},{6,7},{7,6},{8,9},{9,8},{10,11... | collective-permute-start | bytes 98312 | tf_op jit(solution)/shard_map/ppermute | solution.py:337
  0.5 0.9 %load.1 = (bf16[4,16,128]{2,1,0:T(8,128)(2,1)S(1)}, f32[1,1,16,2,128]{4,3,2,1,0:T(2,128)S(1)}, s32[8]{0:T(128)S(4)}, s32[4]{0:T(128)S(4)}, s32[1,1,8]{2,1,0:T(1,128)S(4)}, /*index=5*/s32[1,1,16]{2,1,0:T(1,128)S(4)}) custom-call(f32[4,2048]{1,0:T(4,128)} %refs_0_.1, f32[1,1,16,2,128]{4,3,2,1,0:T(2,128)} %refs_1_.1, s32[8]{0:T(128)} %refs_2_.1, s32[4]{0:T(128)} %refs_3_.1, ...), custom_call_target="tpu_custom_call" | custom-call | tf_op jit(solution)/shard_map/load/pallas_call | solution.py:344
  1.4 0.2 %collective-permute-done.passed = f32[4,2048]{1,0:T(4,128)S(1)} collective-permute-done((f32[4,2048]{1,0:T(4,128)}, f32[4,2048]{1,0:T(4,128)S(1)}, u32[]{:S(2)}, u32[]{:S(2)}) %collective-permute-start) | collective-permute-done | bytes 32800 | tf_op jit(solution)/shard_map/ppermute | solution.py:337
  1.6 3.0 %collective-permute-start.3 = (bf16[2,4,16,128]{3,2,1,0:T(8,128)(2,1)S(1)}, bf16[2,4,16,128]{3,2,1,0:T(8,128)(2,1)S(1)}, u32[]{:S(2)}, u32[]{:S(2)}) collective-permute-start(bf16[2,4,16,128]{3,2,1,0:T(8,128)(2,1)S(1)} %pack.1.refs_0_), channel_id=1, source_target_pairs={{0,8},{1,17},{2,10},{3,19},{4,12},{5,21},{6,14},{7,23},{8,0},{9,25... | collective-permute-start | bytes 98312 | tf_op jit(solution)/shard_map/ppermute | solution.py:337
  4.6 0.1 collective-permute-start.2
  4.6 1.9 %collective-permute-start.1 = (bf16[2,4,16,128]{3,2,1,0:T(8,128)(2,1)S(1)}, bf16[2,4,16,128]{3,2,1,0:T(8,128)(2,1)S(1)}, u32[]{:S(2)}, u32[]{:S(2)}) collective-permute-start(bf16[2,4,16,128]{3,2,1,0:T(8,128)(2,1)S(1)} %pack.1.refs_0_), channel_id=1, source_target_pairs={{0,8},{1,9},{2,10},{3,11},{4,12},{5,13},{6,14},{7,15},{8,0},{9,1},... | collective-permute-start | bytes 98312 | tf_op jit(solution)/shard_map/ppermute | solution.py:337
  7.9 0.2 %column_tables.1 = (bf16[64,256]{1,0:T(8,128)(2,1)S(1)}, f32[2,128,256]{2,1,0:T(8,128)S(1)}, bf16[16,256]{1,0:T(8,128)(2,1)S(1)}) custom-call(s32[8]{0:T(128)S(4)} %get-tuple-element.34.col_off), custom_call_target="tpu_custom_call" | custom-call | tf_op jit(solution)/shard_map/column_tables/pallas_call | solution.py:380
  8.1 0.0 collective-permute-done.3.refs_3_
  8.1 0.4 %collective-permute-done.2.refs_2_ = bf16[2,4,16,128]{3,2,1,0:T(8,128)(2,1)S(1)} collective-permute-done((bf16[2,4,16,128]{3,2,1,0:T(8,128)(2,1)S(1)}, bf16[2,4,16,128]{3,2,1,0:T(8,128)(2,1)S(1)}, u32[]{:S(2)}, u32[]{:S(2)}) %collective-permute-start.2) | collective-permute-done | bytes 32800 | tf_op jit(solution)/shard_map/ppermute | solution.py:337
  8.5 0.4 %collective-permute-done.1.refs_1_ = bf16[2,4,16,128]{3,2,1,0:T(8,128)(2,1)S(1)} collective-permute-done((bf16[2,4,16,128]{3,2,1,0:T(8,128)(2,1)S(1)}, bf16[2,4,16,128]{3,2,1,0:T(8,128)(2,1)S(1)}, u32[]{:S(2)}, u32[]{:S(2)}) %collective-permute-start.1) | collective-permute-done | bytes 32800 | tf_op jit(solution)/shard_map/ppermute | solution.py:337
  8.8 0.6 %bands.1 = (bf16[2,4,16,128]{3,2,1,0:T(8,128)(2,1)S(1)}, bf16[2,4,16,128]{3,2,1,0:T(8,128)(2,1)S(1)}) custom-call(s32[8]{0:T(128)S(4)} %get-tuple-element.34.col_off, bf16[2,4,16,128]{3,2,1,0:T(8,128)(2,1)S(1)} %pack.1.refs_0_, bf16[2,4,16,128]{3,2,1,0:T(8,128)(2,1)S(1)} %collective-permute-done.1.refs_1_, ...), custom_call_target="tpu_custom_call" | custom-call | tf_op jit(solution)/shard_map/bands/pallas_call | solution.py:432
  9.5 1.7 %collective-permute-start.6 = (bf16[2,4,16,128]{3,2,1,0:T(8,128)(2,1)S(1)}, bf16[2,4,16,128]{3,2,1,0:T(8,128)(2,1)S(1)}, u32[]{:S(2)}, u32[]{:S(2)}) collective-permute-start(bf16[2,4,16,128]{3,2,1,0:T(8,128)(2,1)S(1)} %get-tuple-element.40), channel_id=1, source_target_pairs={{0,8},{1,7},{2,10},{3,5},{4,12},{5,3},{6,14},{7,1},{8,0},{9,15},{1... | collective-permute-start | bytes 98312 | tf_op jit(solution)/shard_map/ppermute | solution.py:337
  11.2 0.3 %collective-permute-start.5 = (bf16[2,4,16,128]{3,2,1,0:T(8,128)(2,1)S(1)}, bf16[2,4,16,128]{3,2,1,0:T(8,128)(2,1)S(1)}, u32[]{:S(2)}, u32[]{:S(2)}) collective-permute-start(bf16[2,4,16,128]{3,2,1,0:T(8,128)(2,1)S(1)} %get-tuple-element.40), channel_id=1, source_target_pairs={{0,8},{1,5},{2,10},{3,7},{4,12},{5,1},{6,14},{7,3},{8,0},{9,13},{1... | collective-permute-start | bytes 98312 | tf_op jit(solution)/shard_map/ppermute | solution.py:337
  11.5 1.7 %collective-permute-start.4 = (bf16[2,4,16,128]{3,2,1,0:T(8,128)(2,1)S(1)}, bf16[2,4,16,128]{3,2,1,0:T(8,128)(2,1)S(1)}, u32[]{:S(2)}, u32[]{:S(2)}) collective-permute-start(bf16[2,4,16,128]{3,2,1,0:T(8,128)(2,1)S(1)} %get-tuple-element.45), channel_id=1, source_target_pairs={{0,8},{1,3},{2,10},{3,1},{4,12},{5,7},{6,14},{7,5},{8,0},{9,11},{1... | collective-permute-start | bytes 98312 | tf_op jit(solution)/shard_map/ppermute | solution.py:337
  13.2 1.5 %vis_tables.1 = (f32[2,8,1024]{2,1,0:T(8,128)S(1)}, bf16[16,256,256]{2,1,0:T(8,128)(2,1)S(1)}, f32[16,2,8,128]{3,2,1,0:T(8,128)S(1)}, f32[16,2,16,128]{3,2,1,0:T(8,128)S(1)}, s32[16]{0:T(128)S(4)}) custom-call(s32[4]{0:T(128)S(4)} %get-tuple-element.29.row_off, s32[1,1,8]{2,1,0:T(1,128)S(4)} %get-tuple-element.30.steps, ...), custom_call_target="tpu_custom_call" | custom-call | tf_op jit(solution)/shard_map/vis_tables/pallas_call | solution.py:399
  14.7 0.7 %collective-permute-done.4 = bf16[2,4,16,128]{3,2,1,0:T(8,128)(2,1)S(1)} collective-permute-done((bf16[2,4,16,128]{3,2,1,0:T(8,128)(2,1)S(1)}, bf16[2,4,16,128]{3,2,1,0:T(8,128)(2,1)S(1)}, u32[]{:S(2)}, u32[]{:S(2)}) %collective-permute-start.4) | collective-permute-done | bytes 32800 | tf_op jit(solution)/shard_map/ppermute | solution.py:337
  15.4 0.0 collective-permute-done.6
  15.4 0.0 collective-permute-done.5
  15.5 0.6 %collective-permute-start.7 = (bf16[2,2,4,16,128]{4,3,2,1,0:T(8,128)(2,1)S(1)}, bf16[2,2,4,16,128]{4,3,2,1,0:T(8,128)(2,1)S(1)}, u32[]{:S(2)}, u32[]{:S(2)}) collective-permute-start(bf16[2,2,4,16,128]{4,3,2,1,0:T(8,128)(2,1)S(1)} %pad_maximum_fusion.local), channel_id=1, source_target_pairs={{0,1},{1,0},{2,3},{3,2},{4,5},{5,4},{6,7},{7,6},{8,9},{9,8},{10,11... | collective-permute-start | bytes 196616 | tf_op jit(solution)/shard_map/ppermute | solution.py:337
  16.0 0.9 %collective-permute-done.7.passed = bf16[2,2,4,16,128]{4,3,2,1,0:T(8,128)(2,1)S(1)} collective-permute-done((bf16[2,2,4,16,128]{4,3,2,1,0:T(8,128)(2,1)S(1)}, bf16[2,2,4,16,128]{4,3,2,1,0:T(8,128)(2,1)S(1)}, u32[]{:S(2)}, u32[]{:S(2)}) %collective-permute-start.7) | collective-permute-done | bytes 65568 | tf_op jit(solution)/shard_map/ppermute | solution.py:337
  16.9 1.3 %degrid.1 = f32[1,1,16,2,128]{4,3,2,1,0:T(2,128)} custom-call(s32[16]{0:T(128)S(4)} %get-tuple-element.33.planes, bf16[2,2,4,16,128]{4,3,2,1,0:T(8,128)(2,1)S(1)} %pad_maximum_fusion.local, bf16[2,2,4,16,128]{4,3,2,1,0:T(8,128)(2,1)S(1)} %collective-permute-done.7.passed, f32[2,8,1024]{2,1,0:T(8,128)S(1)} %get-tuple-element.49.cols_tab, ...), custom_call_target="tpu_custom_call" | custom-call | tf_op jit(solution)/shard_map/degrid/pallas_call | solution.py:454
  (4 shorter events, 0.1 us)
Async XLA Ops:
  0.0 1.6 %collective-permute-start = (f32[4,2048]{1,0:T(4,128)}, f32[4,2048]{1,0:T(4,128)S(1)}, u32[]{:S(2)}, u32[]{:S(2)}) collective-permute-start(f32[4,2048]{1,0:T(4,128)} %refs_0_.1), channel_id=1, source_target_pairs={{0,1},{1,0},{2,3},{3,2},{4,5},{5,4},{6,7},{7,6},{8,9},{9,8},{10,11... | collective-permute-start | bytes 98312 | tf_op jit(solution)/shard_map/ppermute | solution.py:337
  1.6 6.5 %collective-permute-start.3 = (bf16[2,4,16,128]{3,2,1,0:T(8,128)(2,1)S(1)}, bf16[2,4,16,128]{3,2,1,0:T(8,128)(2,1)S(1)}, u32[]{:S(2)}, u32[]{:S(2)}) collective-permute-start(bf16[2,4,16,128]{3,2,1,0:T(8,128)(2,1)S(1)} %pack.1.refs_0_), channel_id=1, source_target_pairs={{0,8},{1,17},{2,10},{3,19},{4,12},{5,21},{6,14},{7,23},{8,0},{9,25... | collective-permute-start | bytes 98312 | tf_op jit(solution)/shard_map/ppermute | solution.py:337
  4.6 3.9 %collective-permute-start.2 = (bf16[2,4,16,128]{3,2,1,0:T(8,128)(2,1)S(1)}, bf16[2,4,16,128]{3,2,1,0:T(8,128)(2,1)S(1)}, u32[]{:S(2)}, u32[]{:S(2)}) collective-permute-start(bf16[2,4,16,128]{3,2,1,0:T(8,128)(2,1)S(1)} %pack.1.refs_0_), channel_id=1, source_target_pairs={{0,8},{1,25},{2,10},{3,27},{4,12},{5,29},{6,14},{7,31},{8,0},{9,17... | collective-permute-start | bytes 98312 | tf_op jit(solution)/shard_map/ppermute | solution.py:337
  4.6 4.2 %collective-permute-start.1 = (bf16[2,4,16,128]{3,2,1,0:T(8,128)(2,1)S(1)}, bf16[2,4,16,128]{3,2,1,0:T(8,128)(2,1)S(1)}, u32[]{:S(2)}, u32[]{:S(2)}) collective-permute-start(bf16[2,4,16,128]{3,2,1,0:T(8,128)(2,1)S(1)} %pack.1.refs_0_), channel_id=1, source_target_pairs={{0,8},{1,9},{2,10},{3,11},{4,12},{5,13},{6,14},{7,15},{8,0},{9,1},... | collective-permute-start | bytes 98312 | tf_op jit(solution)/shard_map/ppermute | solution.py:337
  9.5 6.0 %collective-permute-start.6 = (bf16[2,4,16,128]{3,2,1,0:T(8,128)(2,1)S(1)}, bf16[2,4,16,128]{3,2,1,0:T(8,128)(2,1)S(1)}, u32[]{:S(2)}, u32[]{:S(2)}) collective-permute-start(bf16[2,4,16,128]{3,2,1,0:T(8,128)(2,1)S(1)} %get-tuple-element.40), channel_id=1, source_target_pairs={{0,8},{1,7},{2,10},{3,5},{4,12},{5,3},{6,14},{7,1},{8,0},{9,15},{1... | collective-permute-start | bytes 98312 | tf_op jit(solution)/shard_map/ppermute | solution.py:337
  11.2 4.3 %collective-permute-start.5 = (bf16[2,4,16,128]{3,2,1,0:T(8,128)(2,1)S(1)}, bf16[2,4,16,128]{3,2,1,0:T(8,128)(2,1)S(1)}, u32[]{:S(2)}, u32[]{:S(2)}) collective-permute-start(bf16[2,4,16,128]{3,2,1,0:T(8,128)(2,1)S(1)} %get-tuple-element.40), channel_id=1, source_target_pairs={{0,8},{1,5},{2,10},{3,7},{4,12},{5,1},{6,14},{7,3},{8,0},{9,13},{1... | collective-permute-start | bytes 98312 | tf_op jit(solution)/shard_map/ppermute | solution.py:337
  11.5 3.9 %collective-permute-start.4 = (bf16[2,4,16,128]{3,2,1,0:T(8,128)(2,1)S(1)}, bf16[2,4,16,128]{3,2,1,0:T(8,128)(2,1)S(1)}, u32[]{:S(2)}, u32[]{:S(2)}) collective-permute-start(bf16[2,4,16,128]{3,2,1,0:T(8,128)(2,1)S(1)} %get-tuple-element.45), channel_id=1, source_target_pairs={{0,8},{1,3},{2,10},{3,1},{4,12},{5,7},{6,14},{7,5},{8,0},{9,11},{1... | collective-permute-start | bytes 98312 | tf_op jit(solution)/shard_map/ppermute | solution.py:337
  15.5 1.5 %collective-permute-start.7 = (bf16[2,2,4,16,128]{4,3,2,1,0:T(8,128)(2,1)S(1)}, bf16[2,2,4,16,128]{4,3,2,1,0:T(8,128)(2,1)S(1)}, u32[]{:S(2)}, u32[]{:S(2)}) collective-permute-start(bf16[2,2,4,16,128]{4,3,2,1,0:T(8,128)(2,1)S(1)} %pad_maximum_fusion.local), channel_id=1, source_target_pairs={{0,1},{1,0},{2,3},{3,2},{4,5},{5,4},{6,7},{7,6},{8,9},{9,8},{10,11... | collective-permute-start | bytes 196616 | tf_op jit(solution)/shard_map/ppermute | solution.py:337

commit v6 on v5

--- a/solution.py
+++ b/solution.py
@@ -373,7 +373,7 @@
     )(kept(own_sky), kept(passed_sky))
     pieces = [chip_sky]
     for slot in range(1, half_z):
-        pieces.append(exchange(chip_sky, 2 * slot * num_rows, near_flip))
+        pieces.append(exchange(chip_sky, 2 * slot * num_rows, 2))
 
     operands = [pieces[slot] for slot in slot_order(half_z)]
 

time: 18.4 us -> 18.4 us (level)
  no operation moved by 1% of the time
where the time goes in v6:
time: 18.4 us; the launch traced here: 18.2 us
  starting transfers between devices  9.73 us (53%)
  Pallas kernels  4.55 us (25%)
  waiting for transfers between devices  2.53 us (14%)
  between operations  1.35 us (7%)
    ppermute x8, starting transfers between devices, exchange(): return lax.ppermute(value, ('fx', 'fy'), pairs)  9.73 us
    ppermute x8, waiting for transfers between devices, exchange(): return lax.ppermute(value, ('fx', 'fy'), pairs)  2.53 us
    pallas_call x1, Pallas kernels, per_device(): pl.pallas_call(functools.partial(vis_tables_kernel, (half_y, rows_here, n...  1.52 us
    pallas_call x1, Pallas kernels, per_device(): pl.pallas_call(functools.partial(degrid_kernel, (total_rows, SG, blocks,...  1.3 us
    pallas_call x1, Pallas kernels, per_device(): pl.pallas_call(load_kernel, name='load', out_shape=(pltpu.VMEM((rows_here...  0.87 us
    pallas_call x1, Pallas kernels, per_device(): pl.pallas_call(functools.partial(band_kernel, (half_z, facet_rows, fine_c...  0.64 us
  transfers between devices with their start and end apart: 8, of which 5 were waited for; matrix products, arithmetic and copies ran while one was open for 0% of the time, Pallas kernels for 14%

profile of v6, /device:TPU:0, one launch (start us, length us, event | category | flops | bytes accessed | tf_op | source)
XLA Modules:
  0.0 18.2 jit_solution(17116923508248357094)
XLA Ops:
  0.0 0.5 %collective-permute-start = (f32[4,2048]{1,0:T(4,128)}, f32[4,2048]{1,0:T(4,128)S(1)}, u32[]{:S(2)}, u32[]{:S(2)}) collective-permute-start(f32[4,2048]{1,0:T(4,128)} %refs_0_.1), channel_id=1, source_target_pairs={{0,1},{1,0},{2,3},{3,2},{4,5},{5,4},{6,7},{7,6},{8,9},{9,8},{10,11... | collective-permute-start | bytes 98312 | tf_op jit(solution)/shard_map/ppermute | solution.py:337
  0.5 0.9 %load.1 = (bf16[4,16,128]{2,1,0:T(8,128)(2,1)S(1)}, f32[1,1,16,2,128]{4,3,2,1,0:T(2,128)S(1)}, s32[8]{0:T(128)S(4)}, s32[4]{0:T(128)S(4)}, s32[1,1,8]{2,1,0:T(1,128)S(4)}, /*index=5*/s32[1,1,16]{2,1,0:T(1,128)S(4)}) custom-call(f32[4,2048]{1,0:T(4,128)} %refs_0_.1, f32[1,1,16,2,128]{4,3,2,1,0:T(2,128)} %refs_1_.1, s32[8]{0:T(128)} %refs_2_.1, s32[4]{0:T(128)} %refs_3_.1, ...), custom_call_target="tpu_custom_call" | custom-call | tf_op jit(solution)/shard_map/load/pallas_call | solution.py:344
  1.4 0.2 %collective-permute-done.passed = f32[4,2048]{1,0:T(4,128)S(1)} collective-permute-done((f32[4,2048]{1,0:T(4,128)}, f32[4,2048]{1,0:T(4,128)S(1)}, u32[]{:S(2)}, u32[]{:S(2)}) %collective-permute-start) | collective-permute-done | bytes 32800 | tf_op jit(solution)/shard_map/ppermute | solution.py:337
  1.6 2.9 %collective-permute-start.3 = (bf16[2,4,16,128]{3,2,1,0:T(8,128)(2,1)S(1)}, bf16[2,4,16,128]{3,2,1,0:T(8,128)(2,1)S(1)}, u32[]{:S(2)}, u32[]{:S(2)}) collective-permute-start(bf16[2,4,16,128]{3,2,1,0:T(8,128)(2,1)S(1)} %pack.1.refs_0_), channel_id=1, source_target_pairs={{0,2},{1,17},{2,0},{3,19},{4,6},{5,21},{6,4},{7,23},{8,10},{9,25},... | collective-permute-start | bytes 98312 | tf_op jit(solution)/shard_map/ppermute | solution.py:337
  4.5 0.1 collective-permute-start.2
  4.6 1.9 %collective-permute-start.1 = (bf16[2,4,16,128]{3,2,1,0:T(8,128)(2,1)S(1)}, bf16[2,4,16,128]{3,2,1,0:T(8,128)(2,1)S(1)}, u32[]{:S(2)}, u32[]{:S(2)}) collective-permute-start(bf16[2,4,16,128]{3,2,1,0:T(8,128)(2,1)S(1)} %pack.1.refs_0_), channel_id=1, source_target_pairs={{0,2},{1,9},{2,0},{3,11},{4,6},{5,13},{6,4},{7,15},{8,10},{9,1},{1... | collective-permute-start | bytes 98312 | tf_op jit(solution)/shard_map/ppermute | solution.py:337
  7.8 0.2 %column_tables.1 = (bf16[64,256]{1,0:T(8,128)(2,1)S(1)}, f32[2,128,256]{2,1,0:T(8,128)S(1)}, bf16[16,256]{1,0:T(8,128)(2,1)S(1)}) custom-call(s32[8]{0:T(128)S(4)} %get-tuple-element.34.col_off), custom_call_target="tpu_custom_call" | custom-call | tf_op jit(solution)/shard_map/column_tables/pallas_call | solution.py:380
  8.0 0.0 collective-permute-done.3.refs_3_
  8.0 0.4 %collective-permute-done.2.refs_2_ = bf16[2,4,16,128]{3,2,1,0:T(8,128)(2,1)S(1)} collective-permute-done((bf16[2,4,16,128]{3,2,1,0:T(8,128)(2,1)S(1)}, bf16[2,4,16,128]{3,2,1,0:T(8,128)(2,1)S(1)}, u32[]{:S(2)}, u32[]{:S(2)}) %collective-permute-start.2) | collective-permute-done | bytes 32800 | tf_op jit(solution)/shard_map/ppermute | solution.py:337
  8.4 0.4 %collective-permute-done.1.refs_1_ = bf16[2,4,16,128]{3,2,1,0:T(8,128)(2,1)S(1)} collective-permute-done((bf16[2,4,16,128]{3,2,1,0:T(8,128)(2,1)S(1)}, bf16[2,4,16,128]{3,2,1,0:T(8,128)(2,1)S(1)}, u32[]{:S(2)}, u32[]{:S(2)}) %collective-permute-start.1) | collective-permute-done | bytes 32800 | tf_op jit(solution)/shard_map/ppermute | solution.py:337
  8.8 0.6 %bands.1 = (bf16[2,4,16,128]{3,2,1,0:T(8,128)(2,1)S(1)}, bf16[2,4,16,128]{3,2,1,0:T(8,128)(2,1)S(1)}) custom-call(s32[8]{0:T(128)S(4)} %get-tuple-element.34.col_off, bf16[2,4,16,128]{3,2,1,0:T(8,128)(2,1)S(1)} %pack.1.refs_0_, bf16[2,4,16,128]{3,2,1,0:T(8,128)(2,1)S(1)} %collective-permute-done.1.refs_1_, ...), custom_call_target="tpu_custom_call" | custom-call | tf_op jit(solution)/shard_map/bands/pallas_call | solution.py:432
  9.4 1.8 %collective-permute-start.6 = (bf16[2,4,16,128]{3,2,1,0:T(8,128)(2,1)S(1)}, bf16[2,4,16,128]{3,2,1,0:T(8,128)(2,1)S(1)}, u32[]{:S(2)}, u32[]{:S(2)}) collective-permute-start(bf16[2,4,16,128]{3,2,1,0:T(8,128)(2,1)S(1)} %get-tuple-element.40), channel_id=1, source_target_pairs={{0,8},{1,7},{2,10},{3,5},{4,12},{5,3},{6,14},{7,1},{8,0},{9,15},{1... | collective-permute-start | bytes 98312 | tf_op jit(solution)/shard_map/ppermute | solution.py:337
  11.2 0.3 %collective-permute-start.5 = (bf16[2,4,16,128]{3,2,1,0:T(8,128)(2,1)S(1)}, bf16[2,4,16,128]{3,2,1,0:T(8,128)(2,1)S(1)}, u32[]{:S(2)}, u32[]{:S(2)}) collective-permute-start(bf16[2,4,16,128]{3,2,1,0:T(8,128)(2,1)S(1)} %get-tuple-element.40), channel_id=1, source_target_pairs={{0,8},{1,5},{2,10},{3,7},{4,12},{5,1},{6,14},{7,3},{8,0},{9,13},{1... | collective-permute-start | bytes 98312 | tf_op jit(solution)/shard_map/ppermute | solution.py:337
  11.5 1.7 %collective-permute-start.4 = (bf16[2,4,16,128]{3,2,1,0:T(8,128)(2,1)S(1)}, bf16[2,4,16,128]{3,2,1,0:T(8,128)(2,1)S(1)}, u32[]{:S(2)}, u32[]{:S(2)}) collective-permute-start(bf16[2,4,16,128]{3,2,1,0:T(8,128)(2,1)S(1)} %get-tuple-element.45), channel_id=1, source_target_pairs={{0,8},{1,3},{2,10},{3,1},{4,12},{5,7},{6,14},{7,5},{8,0},{9,11},{1... | collective-permute-start | bytes 98312 | tf_op jit(solution)/shard_map/ppermute | solution.py:337
  13.2 1.5 %vis_tables.1 = (f32[2,8,1024]{2,1,0:T(8,128)S(1)}, bf16[16,256,256]{2,1,0:T(8,128)(2,1)S(1)}, f32[16,2,8,128]{3,2,1,0:T(8,128)S(1)}, f32[16,2,16,128]{3,2,1,0:T(8,128)S(1)}, s32[16]{0:T(128)S(4)}) custom-call(s32[4]{0:T(128)S(4)} %get-tuple-element.29.row_off, s32[1,1,8]{2,1,0:T(1,128)S(4)} %get-tuple-element.30.steps, ...), custom_call_target="tpu_custom_call" | custom-call | tf_op jit(solution)/shard_map/vis_tables/pallas_call | solution.py:399
  14.7 0.7 %collective-permute-done.4 = bf16[2,4,16,128]{3,2,1,0:T(8,128)(2,1)S(1)} collective-permute-done((bf16[2,4,16,128]{3,2,1,0:T(8,128)(2,1)S(1)}, bf16[2,4,16,128]{3,2,1,0:T(8,128)(2,1)S(1)}, u32[]{:S(2)}, u32[]{:S(2)}) %collective-permute-start.4) | collective-permute-done | bytes 32800 | tf_op jit(solution)/shard_map/ppermute | solution.py:337
  15.4 0.0 collective-permute-done.6
  15.4 0.0 collective-permute-done.5
  15.5 0.5 %collective-permute-start.7 = (bf16[2,2,4,16,128]{4,3,2,1,0:T(8,128)(2,1)S(1)}, bf16[2,2,4,16,128]{4,3,2,1,0:T(8,128)(2,1)S(1)}, u32[]{:S(2)}, u32[]{:S(2)}) collective-permute-start(bf16[2,2,4,16,128]{4,3,2,1,0:T(8,128)(2,1)S(1)} %pad_maximum_fusion.local), channel_id=1, source_target_pairs={{0,1},{1,0},{2,3},{3,2},{4,5},{5,4},{6,7},{7,6},{8,9},{9,8},{10,11... | collective-permute-start | bytes 196616 | tf_op jit(solution)/shard_map/ppermute | solution.py:337
  16.0 0.9 %collective-permute-done.7.passed = bf16[2,2,4,16,128]{4,3,2,1,0:T(8,128)(2,1)S(1)} collective-permute-done((bf16[2,2,4,16,128]{4,3,2,1,0:T(8,128)(2,1)S(1)}, bf16[2,2,4,16,128]{4,3,2,1,0:T(8,128)(2,1)S(1)}, u32[]{:S(2)}, u32[]{:S(2)}) %collective-permute-start.7) | collective-permute-done | bytes 65568 | tf_op jit(solution)/shard_map/ppermute | solution.py:337
  16.9 1.3 %degrid.1 = f32[1,1,16,2,128]{4,3,2,1,0:T(2,128)} custom-call(s32[16]{0:T(128)S(4)} %get-tuple-element.33.planes, bf16[2,2,4,16,128]{4,3,2,1,0:T(8,128)(2,1)S(1)} %pad_maximum_fusion.local, bf16[2,2,4,16,128]{4,3,2,1,0:T(8,128)(2,1)S(1)} %collective-permute-done.7.passed, f32[2,8,1024]{2,1,0:T(8,128)S(1)} %get-tuple-element.49.cols_tab, ...), custom_call_target="tpu_custom_call" | custom-call | tf_op jit(solution)/shard_map/degrid/pallas_call | solution.py:454
  (4 shorter events, 0.1 us)
Async XLA Ops:
  0.0 1.6 %collective-permute-start = (f32[4,2048]{1,0:T(4,128)}, f32[4,2048]{1,0:T(4,128)S(1)}, u32[]{:S(2)}, u32[]{:S(2)}) collective-permute-start(f32[4,2048]{1,0:T(4,128)} %refs_0_.1), channel_id=1, source_target_pairs={{0,1},{1,0},{2,3},{3,2},{4,5},{5,4},{6,7},{7,6},{8,9},{9,8},{10,11... | collective-permute-start | bytes 98312 | tf_op jit(solution)/shard_map/ppermute | solution.py:337
  1.6 6.5 %collective-permute-start.3 = (bf16[2,4,16,128]{3,2,1,0:T(8,128)(2,1)S(1)}, bf16[2,4,16,128]{3,2,1,0:T(8,128)(2,1)S(1)}, u32[]{:S(2)}, u32[]{:S(2)}) collective-permute-start(bf16[2,4,16,128]{3,2,1,0:T(8,128)(2,1)S(1)} %pack.1.refs_0_), channel_id=1, source_target_pairs={{0,2},{1,17},{2,0},{3,19},{4,6},{5,21},{6,4},{7,23},{8,10},{9,25},... | collective-permute-start | bytes 98312 | tf_op jit(solution)/shard_map/ppermute | solution.py:337
  4.5 3.9 %collective-permute-start.2 = (bf16[2,4,16,128]{3,2,1,0:T(8,128)(2,1)S(1)}, bf16[2,4,16,128]{3,2,1,0:T(8,128)(2,1)S(1)}, u32[]{:S(2)}, u32[]{:S(2)}) collective-permute-start(bf16[2,4,16,128]{3,2,1,0:T(8,128)(2,1)S(1)} %pack.1.refs_0_), channel_id=1, source_target_pairs={{0,2},{1,25},{2,0},{3,27},{4,6},{5,29},{6,4},{7,31},{8,10},{9,17},... | collective-permute-start | bytes 98312 | tf_op jit(solution)/shard_map/ppermute | solution.py:337
  4.6 4.2 %collective-permute-start.1 = (bf16[2,4,16,128]{3,2,1,0:T(8,128)(2,1)S(1)}, bf16[2,4,16,128]{3,2,1,0:T(8,128)(2,1)S(1)}, u32[]{:S(2)}, u32[]{:S(2)}) collective-permute-start(bf16[2,4,16,128]{3,2,1,0:T(8,128)(2,1)S(1)} %pack.1.refs_0_), channel_id=1, source_target_pairs={{0,2},{1,9},{2,0},{3,11},{4,6},{5,13},{6,4},{7,15},{8,10},{9,1},{1... | collective-permute-start | bytes 98312 | tf_op jit(solution)/shard_map/ppermute | solution.py:337
  9.4 6.0 %collective-permute-start.6 = (bf16[2,4,16,128]{3,2,1,0:T(8,128)(2,1)S(1)}, bf16[2,4,16,128]{3,2,1,0:T(8,128)(2,1)S(1)}, u32[]{:S(2)}, u32[]{:S(2)}) collective-permute-start(bf16[2,4,16,128]{3,2,1,0:T(8,128)(2,1)S(1)} %get-tuple-element.40), channel_id=1, source_target_pairs={{0,8},{1,7},{2,10},{3,5},{4,12},{5,3},{6,14},{7,1},{8,0},{9,15},{1... | collective-permute-start | bytes 98312 | tf_op jit(solution)/shard_map/ppermute | solution.py:337
  11.2 4.3 %collective-permute-start.5 = (bf16[2,4,16,128]{3,2,1,0:T(8,128)(2,1)S(1)}, bf16[2,4,16,128]{3,2,1,0:T(8,128)(2,1)S(1)}, u32[]{:S(2)}, u32[]{:S(2)}) collective-permute-start(bf16[2,4,16,128]{3,2,1,0:T(8,128)(2,1)S(1)} %get-tuple-element.40), channel_id=1, source_target_pairs={{0,8},{1,5},{2,10},{3,7},{4,12},{5,1},{6,14},{7,3},{8,0},{9,13},{1... | collective-permute-start | bytes 98312 | tf_op jit(solution)/shard_map/ppermute | solution.py:337
  11.5 4.0 %collective-permute-start.4 = (bf16[2,4,16,128]{3,2,1,0:T(8,128)(2,1)S(1)}, bf16[2,4,16,128]{3,2,1,0:T(8,128)(2,1)S(1)}, u32[]{:S(2)}, u32[]{:S(2)}) collective-permute-start(bf16[2,4,16,128]{3,2,1,0:T(8,128)(2,1)S(1)} %get-tuple-element.45), channel_id=1, source_target_pairs={{0,8},{1,3},{2,10},{3,1},{4,12},{5,7},{6,14},{7,5},{8,0},{9,11},{1... | collective-permute-start | bytes 98312 | tf_op jit(solution)/shard_map/ppermute | solution.py:337
  15.5 1.4 %collective-permute-start.7 = (bf16[2,2,4,16,128]{4,3,2,1,0:T(8,128)(2,1)S(1)}, bf16[2,2,4,16,128]{4,3,2,1,0:T(8,128)(2,1)S(1)}, u32[]{:S(2)}, u32[]{:S(2)}) collective-permute-start(bf16[2,2,4,16,128]{4,3,2,1,0:T(8,128)(2,1)S(1)} %pad_maximum_fusion.local), channel_id=1, source_target_pairs={{0,1},{1,0},{2,3},{3,2},{4,5},{5,4},{6,7},{7,6},{8,9},{9,8},{10,11... | collective-permute-start | bytes 196616 | tf_op jit(solution)/shard_map/ppermute | solution.py:337

commit v7 on v5

--- a/solution.py
+++ b/solution.py
@@ -189,8 +189,13 @@
     squares = centre * centre
     phases = jnp.concatenate([depth * squares for depth in depths], axis=0)
     cosine, sine = turn_of_int(phases, 2 * cols_grid)
-    cols_out[0] = cosine
-    cols_out[1] = sine
+    for layer in range(layers):
+        for part in range(cols_grid // LANES):
+            spot = (slice(layer, layer + 1), slice(part * LANES, (part + 1) * LANES))
+            for side, value in enumerate((cosine, sine)):
+                cols_out[side, layer, part] = jnp.broadcast_to(
+                    value[spot], (rows_grid, LANES)
+                ).astype(jnp.bfloat16)
     fetch.wait()
     coarse_count = cols_grid // LANES
     mids = LANES // FINE
@@ -255,27 +260,15 @@
         strips[pl.ds(index * size, size), :] = jnp.where(
             lead, local[spot].astype(jnp.float32), passed[spot].astype(jnp.float32)
         )
-    for part in range(0, wide, 2):
-        pair = []
-        for col in (part, part + 1):
-            real = strips[pl.ds(col, held, stride=2 * wide), :]
-            imag = strips[pl.ds(wide + col, held, stride=2 * wide), :]
-            pair.append((col, real, imag))
-        rows = pl.ds(part * held, 2 * held)
+    for part in range(wide):
+        real = strips[pl.ds(part, held, stride=2 * wide), :].astype(jnp.bfloat16)
+        imag = strips[pl.ds(wide + part, held, stride=2 * wide), :].astype(jnp.bfloat16)
+        rows = pl.ds(part * held, held)
         for layer in range(layers):
-            turned_real, turned_imag = [], []
-            for col, real, imag in pair:
-                cols = pl.ds(col * LANES, LANES)
-                cosine = cols_tab[0, pl.ds(layer, 1), cols]
-                sine = cols_tab[1, pl.ds(layer, 1), cols]
-                turned_real.append(real * cosine - imag * sine)
-                turned_imag.append(real * sine + imag * cosine)
-            layers_ref[layer, rows, pl.ds(0, LANES)] = jnp.concatenate(turned_real).astype(
-                jnp.bfloat16
-            )
-            layers_ref[layer, rows, pl.ds(LANES, LANES)] = jnp.concatenate(turned_imag).astype(
-                jnp.bfloat16
-            )
+            cosine = cols_tab[0, layer, part]
+            sine = cols_tab[1, layer, part]
+            layers_ref[layer, rows, pl.ds(0, LANES)] = real * cosine - imag * sine
+            layers_ref[layer, rows, pl.ds(LANES, LANES)] = real * sine + imag * cosine
     for block in range(blocks):
         sums = jnp.dot(layers_ref[planes[block]], kernels[block], preferred_element_type=jnp.float32)
         total_real = jnp.zeros((held, LANES), jnp.float32)
@@ -412,7 +405,7 @@
         ),
         name="vis_tables",
         out_shape=(
-            pltpu.VMEM((2, layers, SG), f32),
+            pltpu.VMEM((2, layers, wide, rows_grid, LANES), bf16),
             pltpu.VMEM((blocks, 2 * LANES, 2 * vis_count), bf16),
             pltpu.VMEM((blocks, 2, wide, vis_count), f32),
             pltpu.VMEM((blocks, 2, rows_grid, vis_count), f32),

time: 18.4 us -> 18.4 us (level)
  no operation moved by 1% of the time
where the time goes in v7:
time: 18.4 us; the launch traced here: 18.2 us
  starting transfers between devices  9.77 us (53%)
  Pallas kernels  4.52 us (25%)
  waiting for transfers between devices  2.53 us (14%)
  between operations  1.35 us (7%)
    ppermute x8, starting transfers between devices, exchange(): return lax.ppermute(value, ('fx', 'fy'), pairs)  9.77 us
    ppermute x8, waiting for transfers between devices, exchange(): return lax.ppermute(value, ('fx', 'fy'), pairs)  2.53 us
    pallas_call x1, Pallas kernels, per_device(): pl.pallas_call(functools.partial(vis_tables_kernel, (half_y, rows_here, n...  1.52 us
    pallas_call x1, Pallas kernels, per_device(): pl.pallas_call(functools.partial(degrid_kernel, (total_rows, SG, blocks,...  1.27 us
    pallas_call x1, Pallas kernels, per_device(): pl.pallas_call(load_kernel, name='load', out_shape=(pltpu.VMEM((rows_here...  0.87 us
    pallas_call x1, Pallas kernels, per_device(): pl.pallas_call(functools.partial(band_kernel, (half_z, facet_rows, fine_c...  0.64 us
  transfers between devices with their start and end apart: 8, of which 5 were waited for; matrix products, arithmetic and copies ran while one was open for 0% of the time, Pallas kernels for 14%

profile of v7, /device:TPU:0, one launch (start us, length us, event | category | flops | bytes accessed | tf_op | source)
XLA Modules:
  0.0 18.2 jit_solution(13806031768079250047)
XLA Ops:
  0.0 0.5 %collective-permute-start = (f32[4,2048]{1,0:T(4,128)}, f32[4,2048]{1,0:T(4,128)S(1)}, u32[]{:S(2)}, u32[]{:S(2)}) collective-permute-start(f32[4,2048]{1,0:T(4,128)} %refs_0_.1), channel_id=1, source_target_pairs={{0,1},{1,0},{2,3},{3,2},{4,5},{5,4},{6,7},{7,6},{8,9},{9,8},{10,11... | collective-permute-start | bytes 98312 | tf_op jit(solution)/shard_map/ppermute | solution.py:330
  0.5 0.9 %load.1 = (bf16[4,16,128]{2,1,0:T(8,128)(2,1)S(1)}, f32[1,1,16,2,128]{4,3,2,1,0:T(2,128)S(1)}, s32[8]{0:T(128)S(4)}, s32[4]{0:T(128)S(4)}, s32[1,1,8]{2,1,0:T(1,128)S(4)}, /*index=5*/s32[1,1,16]{2,1,0:T(1,128)S(4)}) custom-call(f32[4,2048]{1,0:T(4,128)} %refs_0_.1, f32[1,1,16,2,128]{4,3,2,1,0:T(2,128)} %refs_1_.1, s32[8]{0:T(128)} %refs_2_.1, s32[4]{0:T(128)} %refs_3_.1, ...), custom_call_target="tpu_custom_call" | custom-call | tf_op jit(solution)/shard_map/load/pallas_call | solution.py:337
  1.4 0.2 %collective-permute-done.passed = f32[4,2048]{1,0:T(4,128)S(1)} collective-permute-done((f32[4,2048]{1,0:T(4,128)}, f32[4,2048]{1,0:T(4,128)S(1)}, u32[]{:S(2)}, u32[]{:S(2)}) %collective-permute-start) | collective-permute-done | bytes 32800 | tf_op jit(solution)/shard_map/ppermute | solution.py:330
  1.6 3.0 %collective-permute-start.3 = (bf16[2,4,16,128]{3,2,1,0:T(8,128)(2,1)S(1)}, bf16[2,4,16,128]{3,2,1,0:T(8,128)(2,1)S(1)}, u32[]{:S(2)}, u32[]{:S(2)}) collective-permute-start(bf16[2,4,16,128]{3,2,1,0:T(8,128)(2,1)S(1)} %pack.1.refs_0_), channel_id=1, source_target_pairs={{0,8},{1,17},{2,10},{3,19},{4,12},{5,21},{6,14},{7,23},{8,0},{9,25... | collective-permute-start | bytes 98312 | tf_op jit(solution)/shard_map/ppermute | solution.py:330
  4.6 0.1 collective-permute-start.2
  4.6 1.9 %collective-permute-start.1 = (bf16[2,4,16,128]{3,2,1,0:T(8,128)(2,1)S(1)}, bf16[2,4,16,128]{3,2,1,0:T(8,128)(2,1)S(1)}, u32[]{:S(2)}, u32[]{:S(2)}) collective-permute-start(bf16[2,4,16,128]{3,2,1,0:T(8,128)(2,1)S(1)} %pack.1.refs_0_), channel_id=1, source_target_pairs={{0,8},{1,9},{2,10},{3,11},{4,12},{5,13},{6,14},{7,15},{8,0},{9,1},... | collective-permute-start | bytes 98312 | tf_op jit(solution)/shard_map/ppermute | solution.py:330
  7.9 0.2 %column_tables.1 = (bf16[64,256]{1,0:T(8,128)(2,1)S(1)}, f32[2,128,256]{2,1,0:T(8,128)S(1)}, bf16[16,256]{1,0:T(8,128)(2,1)S(1)}) custom-call(s32[8]{0:T(128)S(4)} %get-tuple-element.34.col_off), custom_call_target="tpu_custom_call" | custom-call | tf_op jit(solution)/shard_map/column_tables/pallas_call | solution.py:373
  8.1 0.0 collective-permute-done.3.refs_3_
  8.1 0.4 %collective-permute-done.2.refs_2_ = bf16[2,4,16,128]{3,2,1,0:T(8,128)(2,1)S(1)} collective-permute-done((bf16[2,4,16,128]{3,2,1,0:T(8,128)(2,1)S(1)}, bf16[2,4,16,128]{3,2,1,0:T(8,128)(2,1)S(1)}, u32[]{:S(2)}, u32[]{:S(2)}) %collective-permute-start.2) | collective-permute-done | bytes 32800 | tf_op jit(solution)/shard_map/ppermute | solution.py:330
  8.5 0.4 %collective-permute-done.1.refs_1_ = bf16[2,4,16,128]{3,2,1,0:T(8,128)(2,1)S(1)} collective-permute-done((bf16[2,4,16,128]{3,2,1,0:T(8,128)(2,1)S(1)}, bf16[2,4,16,128]{3,2,1,0:T(8,128)(2,1)S(1)}, u32[]{:S(2)}, u32[]{:S(2)}) %collective-permute-start.1) | collective-permute-done | bytes 32800 | tf_op jit(solution)/shard_map/ppermute | solution.py:330
  8.8 0.6 %bands.1 = (bf16[2,4,16,128]{3,2,1,0:T(8,128)(2,1)S(1)}, bf16[2,4,16,128]{3,2,1,0:T(8,128)(2,1)S(1)}) custom-call(s32[8]{0:T(128)S(4)} %get-tuple-element.34.col_off, bf16[2,4,16,128]{3,2,1,0:T(8,128)(2,1)S(1)} %pack.1.refs_0_, bf16[2,4,16,128]{3,2,1,0:T(8,128)(2,1)S(1)} %collective-permute-done.1.refs_1_, ...), custom_call_target="tpu_custom_call" | custom-call | tf_op jit(solution)/shard_map/bands/pallas_call | solution.py:425
  9.5 1.7 %collective-permute-start.6 = (bf16[2,4,16,128]{3,2,1,0:T(8,128)(2,1)S(1)}, bf16[2,4,16,128]{3,2,1,0:T(8,128)(2,1)S(1)}, u32[]{:S(2)}, u32[]{:S(2)}) collective-permute-start(bf16[2,4,16,128]{3,2,1,0:T(8,128)(2,1)S(1)} %get-tuple-element.40), channel_id=1, source_target_pairs={{0,8},{1,7},{2,10},{3,5},{4,12},{5,3},{6,14},{7,1},{8,0},{9,15},{1... | collective-permute-start | bytes 98312 | tf_op jit(solution)/shard_map/ppermute | solution.py:330
  11.2 0.3 %collective-permute-start.5 = (bf16[2,4,16,128]{3,2,1,0:T(8,128)(2,1)S(1)}, bf16[2,4,16,128]{3,2,1,0:T(8,128)(2,1)S(1)}, u32[]{:S(2)}, u32[]{:S(2)}) collective-permute-start(bf16[2,4,16,128]{3,2,1,0:T(8,128)(2,1)S(1)} %get-tuple-element.40), channel_id=1, source_target_pairs={{0,8},{1,5},{2,10},{3,7},{4,12},{5,1},{6,14},{7,3},{8,0},{9,13},{1... | collective-permute-start | bytes 98312 | tf_op jit(solution)/shard_map/ppermute | solution.py:330
  11.5 1.7 %collective-permute-start.4 = (bf16[2,4,16,128]{3,2,1,0:T(8,128)(2,1)S(1)}, bf16[2,4,16,128]{3,2,1,0:T(8,128)(2,1)S(1)}, u32[]{:S(2)}, u32[]{:S(2)}) collective-permute-start(bf16[2,4,16,128]{3,2,1,0:T(8,128)(2,1)S(1)} %get-tuple-element.45), channel_id=1, source_target_pairs={{0,8},{1,3},{2,10},{3,1},{4,12},{5,7},{6,14},{7,5},{8,0},{9,11},{1... | collective-permute-start | bytes 98312 | tf_op jit(solution)/shard_map/ppermute | solution.py:330
  13.2 1.5 %vis_tables.1 = (bf16[2,8,8,16,128]{4,3,2,1,0:T(8,128)(2,1)S(1)}, bf16[16,256,256]{2,1,0:T(8,128)(2,1)S(1)}, f32[16,2,8,128]{3,2,1,0:T(8,128)S(1)}, f32[16,2,16,128]{3,2,1,0:T(8,128)S(1)}, s32[16]{0:T(128)S(4)}) custom-call(s32[4]{0:T(128)S(4)} %get-tuple-element.29.row_off, s32[1,1,8]{2,1,0:T(1,128)S(4)} %get-tuple-element.30.steps, ...), custom_call_target="tpu_custom_call" | custom-call | tf_op jit(solution)/shard_map/vis_tables/pallas_call | solution.py:392
  14.7 0.7 %collective-permute-done.4 = bf16[2,4,16,128]{3,2,1,0:T(8,128)(2,1)S(1)} collective-permute-done((bf16[2,4,16,128]{3,2,1,0:T(8,128)(2,1)S(1)}, bf16[2,4,16,128]{3,2,1,0:T(8,128)(2,1)S(1)}, u32[]{:S(2)}, u32[]{:S(2)}) %collective-permute-start.4) | collective-permute-done | bytes 32800 | tf_op jit(solution)/shard_map/ppermute | solution.py:330
  15.4 0.0 collective-permute-done.6
  15.4 0.0 collective-permute-done.5
  15.5 0.6 %collective-permute-start.7 = (bf16[2,2,4,16,128]{4,3,2,1,0:T(8,128)(2,1)S(1)}, bf16[2,2,4,16,128]{4,3,2,1,0:T(8,128)(2,1)S(1)}, u32[]{:S(2)}, u32[]{:S(2)}) collective-permute-start(bf16[2,2,4,16,128]{4,3,2,1,0:T(8,128)(2,1)S(1)} %pad_maximum_fusion.local), channel_id=1, source_target_pairs={{0,1},{1,0},{2,3},{3,2},{4,5},{5,4},{6,7},{7,6},{8,9},{9,8},{10,11... | collective-permute-start | bytes 196616 | tf_op jit(solution)/shard_map/ppermute | solution.py:330
  16.0 0.9 %collective-permute-done.7.passed = bf16[2,2,4,16,128]{4,3,2,1,0:T(8,128)(2,1)S(1)} collective-permute-done((bf16[2,2,4,16,128]{4,3,2,1,0:T(8,128)(2,1)S(1)}, bf16[2,2,4,16,128]{4,3,2,1,0:T(8,128)(2,1)S(1)}, u32[]{:S(2)}, u32[]{:S(2)}) %collective-permute-start.7) | collective-permute-done | bytes 65568 | tf_op jit(solution)/shard_map/ppermute | solution.py:330
  16.9 1.3 %degrid.1 = f32[1,1,16,2,128]{4,3,2,1,0:T(2,128)} custom-call(s32[16]{0:T(128)S(4)} %get-tuple-element.33.planes, bf16[2,2,4,16,128]{4,3,2,1,0:T(8,128)(2,1)S(1)} %pad_maximum_fusion.local, bf16[2,2,4,16,128]{4,3,2,1,0:T(8,128)(2,1)S(1)} %collective-permute-done.7.passed, bf16[2,8,8,16,128]{4,3,2,1,0:T(8,128)(2,1)S(1)} %get-tuple-element.49.cols_tab, ...), custom_call_target="tpu_custom_call" | custom-call | tf_op jit(solution)/shard_map/degrid/pallas_call | solution.py:447
  (4 shorter events, 0.1 us)
Async XLA Ops:
  0.0 1.6 %collective-permute-start = (f32[4,2048]{1,0:T(4,128)}, f32[4,2048]{1,0:T(4,128)S(1)}, u32[]{:S(2)}, u32[]{:S(2)}) collective-permute-start(f32[4,2048]{1,0:T(4,128)} %refs_0_.1), channel_id=1, source_target_pairs={{0,1},{1,0},{2,3},{3,2},{4,5},{5,4},{6,7},{7,6},{8,9},{9,8},{10,11... | collective-permute-start | bytes 98312 | tf_op jit(solution)/shard_map/ppermute | solution.py:330
  1.6 6.5 %collective-permute-start.3 = (bf16[2,4,16,128]{3,2,1,0:T(8,128)(2,1)S(1)}, bf16[2,4,16,128]{3,2,1,0:T(8,128)(2,1)S(1)}, u32[]{:S(2)}, u32[]{:S(2)}) collective-permute-start(bf16[2,4,16,128]{3,2,1,0:T(8,128)(2,1)S(1)} %pack.1.refs_0_), channel_id=1, source_target_pairs={{0,8},{1,17},{2,10},{3,19},{4,12},{5,21},{6,14},{7,23},{8,0},{9,25... | collective-permute-start | bytes 98312 | tf_op jit(solution)/shard_map/ppermute | solution.py:330
  4.6 3.9 %collective-permute-start.2 = (bf16[2,4,16,128]{3,2,1,0:T(8,128)(2,1)S(1)}, bf16[2,4,16,128]{3,2,1,0:T(8,128)(2,1)S(1)}, u32[]{:S(2)}, u32[]{:S(2)}) collective-permute-start(bf16[2,4,16,128]{3,2,1,0:T(8,128)(2,1)S(1)} %pack.1.refs_0_), channel_id=1, source_target_pairs={{0,8},{1,25},{2,10},{3,27},{4,12},{5,29},{6,14},{7,31},{8,0},{9,17... | collective-permute-start | bytes 98312 | tf_op jit(solution)/shard_map/ppermute | solution.py:330
  4.6 4.2 %collective-permute-start.1 = (bf16[2,4,16,128]{3,2,1,0:T(8,128)(2,1)S(1)}, bf16[2,4,16,128]{3,2,1,0:T(8,128)(2,1)S(1)}, u32[]{:S(2)}, u32[]{:S(2)}) collective-permute-start(bf16[2,4,16,128]{3,2,1,0:T(8,128)(2,1)S(1)} %pack.1.refs_0_), channel_id=1, source_target_pairs={{0,8},{1,9},{2,10},{3,11},{4,12},{5,13},{6,14},{7,15},{8,0},{9,1},... | collective-permute-start | bytes 98312 | tf_op jit(solution)/shard_map/ppermute | solution.py:330
  9.5 6.0 %collective-permute-start.6 = (bf16[2,4,16,128]{3,2,1,0:T(8,128)(2,1)S(1)}, bf16[2,4,16,128]{3,2,1,0:T(8,128)(2,1)S(1)}, u32[]{:S(2)}, u32[]{:S(2)}) collective-permute-start(bf16[2,4,16,128]{3,2,1,0:T(8,128)(2,1)S(1)} %get-tuple-element.40), channel_id=1, source_target_pairs={{0,8},{1,7},{2,10},{3,5},{4,12},{5,3},{6,14},{7,1},{8,0},{9,15},{1... | collective-permute-start | bytes 98312 | tf_op jit(solution)/shard_map/ppermute | solution.py:330
  11.2 4.3 %collective-permute-start.5 = (bf16[2,4,16,128]{3,2,1,0:T(8,128)(2,1)S(1)}, bf16[2,4,16,128]{3,2,1,0:T(8,128)(2,1)S(1)}, u32[]{:S(2)}, u32[]{:S(2)}) collective-permute-start(bf16[2,4,16,128]{3,2,1,0:T(8,128)(2,1)S(1)} %get-tuple-element.40), channel_id=1, source_target_pairs={{0,8},{1,5},{2,10},{3,7},{4,12},{5,1},{6,14},{7,3},{8,0},{9,13},{1... | collective-permute-start | bytes 98312 | tf_op jit(solution)/shard_map/ppermute | solution.py:330
  11.5 3.9 %collective-permute-start.4 = (bf16[2,4,16,128]{3,2,1,0:T(8,128)(2,1)S(1)}, bf16[2,4,16,128]{3,2,1,0:T(8,128)(2,1)S(1)}, u32[]{:S(2)}, u32[]{:S(2)}) collective-permute-start(bf16[2,4,16,128]{3,2,1,0:T(8,128)(2,1)S(1)} %get-tuple-element.45), channel_id=1, source_target_pairs={{0,8},{1,3},{2,10},{3,1},{4,12},{5,7},{6,14},{7,5},{8,0},{9,11},{1... | collective-permute-start | bytes 98312 | tf_op jit(solution)/shard_map/ppermute | solution.py:330
  15.5 1.5 %collective-permute-start.7 = (bf16[2,2,4,16,128]{4,3,2,1,0:T(8,128)(2,1)S(1)}, bf16[2,2,4,16,128]{4,3,2,1,0:T(8,128)(2,1)S(1)}, u32[]{:S(2)}, u32[]{:S(2)}) collective-permute-start(bf16[2,2,4,16,128]{4,3,2,1,0:T(8,128)(2,1)S(1)} %pad_maximum_fusion.local), channel_id=1, source_target_pairs={{0,1},{1,0},{2,3},{3,2},{4,5},{5,4},{6,7},{7,6},{8,9},{9,8},{10,11... | collective-permute-start | bytes 196616 | tf_op jit(solution)/shard_map/ppermute | solution.py:330
